TPU v7x, 512 devices: a whole 4x8x8 slice. The times are simulated.
512 devices in a mesh: section: 4 (over x), ctx: 64 (over z, y), tp: 2 (over core).
Axes of the slice: x: 4, y: 8, z: 8, core: 2. Of those that a mesh axis runs over, the one named last changes fastest.
Arguments:
- section_input: float32 [4, 8192, 4096], P('section', 'ctx', 'tp'), may hold values from -60 to 60
- long_filter: bfloat16 [4, 8192, 256], P('section', 'ctx', 'tp'), may hold values from -2 to 2
- short_filter: bfloat16 [4, 3, 3, 4096], P('section', None, None, 'tp'), may hold values from -12 to 12
- skip_gain: float32 [4, 4096], P('section', 'tp'), may hold values from -1 to 1
Outputs:
- received: float32 [4, 8192, 4096], P('section', 'ctx', 'tp')
All inputs are finite; a program needn't handle non-finite values.
Results may differ from a plain program's by a relative error of at most 0.009.
Values may be sent and summed in bfloat16 or wider, within the bound.
A program may use at most 64 MiB of HBM per device.

v0:
```python
import jax
import jax.numpy as jnp
import numpy as np
from jax import lax
from jax.sharding import PartitionSpec as P

CHAN = 4096
GROUP = 16
TAPS = 3
BLOCK = 128
SEQ = 8192
HALF = SEQ // BLOCK
SPAN = 2 * HALF
TOTAL = SPAN * BLOCK
ROWS = HALF + 1


def unit_pair(position, period):
    mirror = period - position
    folded = np.minimum(position, mirror)
    angle = folded.astype(np.float32) * np.float32(2 * np.pi / period)
    cosine = np.where(4 * folded == period, 0.0, np.cos(angle)).astype(np.float32)
    sine = np.where((folded == 0) | (2 * folded == period), 0.0, np.sin(angle)).astype(np.float32)
    sine = np.where(position > mirror, -sine, sine)
    return cosine, -sine


def tables():
    k1 = np.arange(ROWS)
    a = np.arange(HALF)
    b = np.arange(BLOCK)
    outer = unit_pair(k1[:, None] * a[None, :] % SPAN, SPAN)
    inner = unit_pair(b[:, None] * b[None, :] % BLOCK, BLOCK)
    turn = unit_pair(k1[:, None] * b[None, :] % TOTAL, TOTAL)
    return outer, inner, turn


def from_behind(block, axis, distance):
    devices = range(lax.axis_size(axis))
    route = [(i - distance, i) for i in devices if i - distance in devices]
    return lax.ppermute(block, axis, route)


def passed_along(x, axis, by):
    peers = lax.axis_size(axis)
    return lax.ppermute(x, axis, [(i, (i + by) % peers) for i in range(peers)])


def rotate(turn_re, turn_im, re, im):
    return (
        (turn_re * re - turn_im * im).astype(jnp.bfloat16),
        (turn_re * im + turn_im * re).astype(jnp.bfloat16),
    )


def dot32(form, left, right):
    return jnp.einsum(form, left, right, preferred_element_type=jnp.float32)


def convolve(signal, kernel):
    channels = signal.shape[1]
    filters = kernel.shape[1]
    (outer_re, outer_im), (inner_re, inner_im), (turn_re, turn_im) = tables()
    outer = jnp.asarray(np.concatenate([outer_re, outer_im]), jnp.bfloat16)
    forward = jnp.asarray(np.block([[inner_re, inner_im], [-inner_im, inner_re]]), jnp.bfloat16)
    inverse = jnp.asarray(np.block([[inner_re, -inner_im], [inner_im, inner_re]]), jnp.bfloat16)
    turn_re = turn_re[:, None, :]
    turn_im = turn_im[:, None, :]
    data = jnp.concatenate([signal, kernel], axis=1)
    first = dot32("ka,acb->kcb", outer, data).astype(jnp.bfloat16).astype(jnp.float32)
    turned = rotate(turn_re, turn_im, first[:ROWS], first[ROWS:])
    spec = dot32("kcb,bq->kcq", jnp.concatenate(turned, axis=2), forward)
    spec_re, spec_im = spec[..., :BLOCK], spec[..., BLOCK:]
    filt_re = jnp.repeat(spec_re[:, channels:], channels // filters, axis=1)
    filt_im = jnp.repeat(spec_im[:, channels:], channels // filters, axis=1)
    weighted = rotate(filt_re, filt_im, spec_re[:, :channels], spec_im[:, :channels])
    back = dot32("kcq,qb->kcb", jnp.concatenate(weighted, axis=2), inverse)
    unturned = rotate(turn_re, -turn_im, back[..., :BLOCK], back[..., BLOCK:])
    fold = np.full((ROWS, 1), 2.0, np.float32)
    fold[0] = fold[-1] = 1.0
    final = jnp.asarray(np.concatenate([outer_re * fold, outer_im * fold]), jnp.bfloat16)
    conv = dot32("ka,kcb->acb", final, jnp.concatenate(unturned, axis=0))
    return (conv * (1.0 / TOTAL)).astype(jnp.bfloat16)


def local(section_input, long_filter, short_filter, skip_gain):
    acts_local = section_input[0]
    tok_rows, chan_local = acts_local.shape
    filt_local = long_filter.shape[2]
    n_ctx = lax.axis_size("ctx")
    partial_squares = jnp.sum(acts_local * acts_local, axis=1)
    total_squares = lax.psum(partial_squares, "tp")
    normed = (acts_local * lax.rsqrt(total_squares / CHAN + 1e-06)[:, None]).astype(jnp.bfloat16)
    earlier = from_behind(normed[tok_rows - (TAPS - 1) :], "ctx", 1)
    extended = jnp.concatenate([earlier, normed], axis=0)
    taps_all = short_filter[0].astype(jnp.float32)
    featured = []
    for feature_id in range(3):
        running = jnp.zeros((tok_rows, chan_local), jnp.float32)
        for offset in range(TAPS):
            begin_row = TAPS - 1 - offset
            running = (
                running
                + taps_all[feature_id, offset][None, :] * extended[begin_row : begin_row + tok_rows]
            )
        featured.append(running)
    query = featured[0].astype(jnp.bfloat16)
    product = (featured[1] * featured[2]).astype(jnp.bfloat16)
    signal = product.T.reshape(n_ctx, chan_local // n_ctx, BLOCK)
    kernel = long_filter[0].T.reshape(n_ctx, filt_local // n_ctx, BLOCK)
    signal = lax.all_to_all(signal, "ctx", split_axis=0, concat_axis=0, tiled=True)
    kernel = lax.all_to_all(kernel, "ctx", split_axis=0, concat_axis=0, tiled=True)
    conv = convolve(signal, kernel)
    conv = lax.all_to_all(conv, "ctx", split_axis=0, concat_axis=0, tiled=True)
    conv_tokens = conv.reshape(chan_local, BLOCK).T
    finished = acts_local + query.astype(jnp.float32) * (
        conv_tokens.astype(jnp.float32) + skip_gain[0][None, :] * product.astype(jnp.float32)
    )
    received = passed_along(finished.astype(jnp.bfloat16), "section", 1).astype(finished.dtype)
    return received[None]


def solution(mesh):
    in_specs = (
        P("section", "ctx", "tp"),
        P("section", "ctx", "tp"),
        P("section", None, None, "tp"),
        P("section", "tp"),
    )
    out_specs = P("section", "ctx", "tp")
    return jax.shard_map(local, mesh=mesh, in_specs=in_specs, out_specs=out_specs, check_vma=False)
```

profile of v0, /device:TPU:16, one launch (start us, length us, event | category | flops | bytes accessed | tf_op | source)
XLA Modules:
  0.0 122.1 jit_solution(3310373822935346058)
XLA Ops:
  0.0 1.5 %copy.23 = bf16[1,128,128]{1,2,0:T(8,128)(2,1)} copy(bf16[1,128,128]{2,1,0:T(8,128)(2,1)} %param.12) | data formatting | bytes 65536 | tf_op args[1]
  1.5 16.5 %all-to-all-start.1 = ((bf16[64,2,128]{2,1,0:T(2,128)(2,1)}), bf16[64,2,128]{2,1,0:T(2,128)(2,1)S(1)}, u32[]{:S(2)}, u32[]{:S(2)}) async-start(bf16[64,2,128]{2,1,0:T(2,128)(2,1)} %bitcast.16), calls=%async_computation.1 | async-start | bytes 65536 | tf_op jit(solution)/shard_map/all_to_all | solution.py:112
  17.9 1.6 %copy.22 = f32[1,128,2048]{1,2,0:T(8,128)S(1)} copy(f32[1,128,2048]{2,1,0:T(8,128)} %param.11) | data formatting | bytes 2097152 | tf_op args[0]
  19.8 2.5 %psum.7 = f32[128]{0:T(128)S(1)} all-reduce(f32[128]{0:T(128)S(1)} %fusion.26), channel_id=1, replica_groups=mesh['section'=4,'ctx'=64,'tp'=2] {'tp'}, use_global_device_ids=true, to_apply=%region_1.0 | all-reduce | flops 128 | bytes 1024 | tf_op jit(solution)/shard_map/psum | solution.py:92
  22.5 3.4 %collective-permute-start = (bf16[2,2048]{0,1:T(8,128)(2,1)S(1)}, bf16[2,2048]{0,1:T(8,128)(2,1)S(1)}, u32[]{:S(2)}, u32[]{:S(2)}) collective-permute-start(bf16[2,2048]{0,1:T(8,128)(2,1)S(1)} %slice.92), channel_id=1, source_target_pairs={{0,2},{2,4},{4,6},{6,8},{8,10},{10,12},{12,14},{14,16},{16,18},{18... | collective-permute-start | bytes 24584 | tf_op jit(solution)/shard_map/ppermute | solution.py:41
  26.0 12.4 %collective-permute-done = bf16[2,2048]{0,1:T(8,128)(2,1)S(1)} collective-permute-done((bf16[2,2048]{0,1:T(8,128)(2,1)S(1)}, bf16[2,2048]{0,1:T(8,128)(2,1)S(1)}, u32[]{:S(2)}, u32[]{:S(2)}) %collective-permute-start) | collective-permute-done | bytes 8224 | tf_op jit(solution)/shard_map/ppermute | solution.py:41
  38.4 3.1 %fusion.19 = bf16[128,2048]{0,1:T(8,128)(2,1)} fusion(bf16[128,2048]{0,1:T(8,128)(2,1)S(1)} %fusion.27, f32[2048]{0:T(1024)S(1)} %bitcast.78, f32[2048]{0:T(1024)S(1)} %bitcast.79, f32[2048]{0:T(1024)S(1)} %bitcast.80, f32[2048]{0:T(1024)S(1)} %bitcast.81, f32[2048]{0:T(1024)S(1)} %bitcast.82, f32[2048]{0:T(1024)S(1)} %bitcast.83, ...), kind=kLoop, calls=%fused_computation.41 | loop fusion | flops 5505024 | bytes 1105920 | tf_op jit(solution)/shard_map/convert_element_type | solution.py:108
  41.5 14.0 %all-to-all-start = ((bf16[64,32,128]{2,1,0:T(8,128)(2,1)}), bf16[64,32,128]{2,1,0:T(8,128)(2,1)S(1)}, u32[]{:S(2)}, u32[]{:S(2)}) async-start(bf16[64,32,128]{2,1,0:T(8,128)(2,1)} %bitcast.13), calls=%async_computation | async-start | bytes 1048576 | tf_op jit(solution)/shard_map/all_to_all | solution.py:111
  55.6 18.4 %all-to-all-done = bf16[64,32,128]{2,1,0:T(8,128)(2,1)S(1)} async-done(((bf16[64,32,128]{2,1,0:T(8,128)(2,1)}), bf16[64,32,128]{2,1,0:T(8,128)(2,1)S(1)}, u32[]{:S(2)}, u32[]{:S(2)}) %all-to-all-start) | async-done | bytes 524320 | tf_op jit(solution)/shard_map/all_to_all | solution.py:111
  74.3 0.5 convert_bitcast_fusion
  75.0 0.4 subtract_convert_fusion
  75.5 0.5 copy-done.2
  75.9 0.5 fusion.1
  76.9 0.8 copy-done.1
  77.7 0.4 fusion.11
  78.1 0.3 copy-done.4
  78.8 0.6 copy-done.8
  79.5 0.5 fusion.5
  80.0 0.3 copy.28
  80.4 23.4 %all_to_all.15 = bf16[64,32,128]{2,1,0:T(8,128)(2,1)S(1)} all-to-all(bf16[64,32,128]{2,1,0:T(8,128)(2,1)S(1)} %copy.28), channel_id=1, replica_groups=mesh['section'=4,'ctx'=64,'tp'=2] {'ctx'}, dimensions={0} | all-to-all | bytes 1048576 | tf_op jit(solution)/shard_map/all_to_all | solution.py:114
  103.8 3.3 %fusion.25 = bf16[128,2048]{0,1:T(8,128)(2,1)S(1)} fusion(f32[1,128,2048]{1,2,0:T(8,128)S(1)} %copy.22, bf16[128,2048]{0,1:T(8,128)(2,1)} %fusion.19, bf16[128,2048]{0,1:T(8,128)(2,1)S(1)} %fusion.27, bf16[64,32,128]{2,1,0:T(8,128)(2,1)S(1)} %all_to_all.15, f32[2048]{0:T(1024)S(1)} %bitcast.84, f32[2048]{0:T(1024)S(1)} %bitcast.76, f32[2048]{0:T(1024)S(1)} %bitcast.77, ...), kind=kLoop, calls=%fused_computation.50 | loop fusion | flops 6029312 | bytes 3186688 | tf_op jit(solution)/shard_map/convert_element_type | solution.py:119
  107.0 3.4 %collective-permute-start.1 = (bf16[128,2048]{0,1:T(8,128)(2,1)S(1)}, bf16[128,2048]{0,1:T(8,128)(2,1)S(1)}, u32[]{:S(2)}, u32[]{:S(2)}) collective-permute-start(bf16[128,2048]{0,1:T(8,128)(2,1)S(1)} %fusion.25), channel_id=1, source_target_pairs={{0,128},{128,256},{256,384},{384,0},{1,129},{129,257},{257,385},{3... | collective-permute-start | bytes 1572872 | tf_op jit(solution)/shard_map/ppermute | solution.py:46
  110.4 10.3 %collective-permute-done.1 = bf16[128,2048]{0,1:T(8,128)(2,1)S(1)} collective-permute-done((bf16[128,2048]{0,1:T(8,128)(2,1)S(1)}, bf16[128,2048]{0,1:T(8,128)(2,1)S(1)}, u32[]{:S(2)}, u32[]{:S(2)}) %collective-permute-start.1) | collective-permute-done | bytes 524320 | tf_op jit(solution)/shard_map/ppermute | solution.py:46
  120.8 1.3 %copy.29 = f32[1,128,2048]{2,1,0:T(8,128)} copy(f32[1,128,2048]{1,2,0:T(8,128)S(1)} %bitcast_convert_fusion) | data formatting | bytes 2097152 | tf_op jit(solution)/shard_map/broadcast_in_dim | solution.py:120
  (29 shorter events, 2.0 us)
Async XLA Ops:
  1.5 40.0 %all-to-all-start.1 = ((bf16[64,2,128]{2,1,0:T(2,128)(2,1)}), bf16[64,2,128]{2,1,0:T(2,128)(2,1)S(1)}, u32[]{:S(2)}, u32[]{:S(2)}) async-start(bf16[64,2,128]{2,1,0:T(2,128)(2,1)} %bitcast.16), calls=%async_computation.1 | async-start | bytes 65536 | tf_op jit(solution)/shard_map/all_to_all | solution.py:112
  22.3 3.7 %copy-start.3 = (bf16[1,3,3,2048]{3,2,1,0:T(4,128)(2,1)S(1)}, bf16[1,3,3,2048]{3,2,1,0:T(4,128)(2,1)}, u32[]{:S(2)}) copy-start(bf16[1,3,3,2048]{3,2,1,0:T(4,128)(2,1)} %param.13) | copy-start | bytes 110596
  22.5 15.9 %collective-permute-start = (bf16[2,2048]{0,1:T(8,128)(2,1)S(1)}, bf16[2,2048]{0,1:T(8,128)(2,1)S(1)}, u32[]{:S(2)}, u32[]{:S(2)}) collective-permute-start(bf16[2,2048]{0,1:T(8,128)(2,1)S(1)} %slice.92), channel_id=1, source_target_pairs={{0,2},{2,4},{4,6},{6,8},{8,10},{10,12},{12,14},{14,16},{16,18},{18... | collective-permute-start | bytes 24584 | tf_op jit(solution)/shard_map/ppermute | solution.py:41
  41.5 32.7 %copy-start.6 = (bf16[130,64,1]{0,1,2:T(8,128)(2,1)S(1)}, bf16[130,64,1]{0,1,2:T(8,128)(2,1)}, u32[]{:S(2)}) copy-start(bf16[130,64,1]{0,1,2:T(8,128)(2,1)} %constant.37) | copy-start | bytes 49924
  41.5 32.5 %all-to-all-start = ((bf16[64,32,128]{2,1,0:T(8,128)(2,1)}), bf16[64,32,128]{2,1,0:T(8,128)(2,1)S(1)}, u32[]{:S(2)}, u32[]{:S(2)}) async-start(bf16[64,32,128]{2,1,0:T(8,128)(2,1)} %bitcast.13), calls=%async_computation | async-start | bytes 1048576 | tf_op jit(solution)/shard_map/all_to_all | solution.py:111
  74.2 0.8 copy-start
  74.2 0.8 copy-start.5
  75.0 0.9 copy-start.2
  76.8 0.9 copy-start.1
  77.7 0.8 copy-start.4
  78.7 0.8 copy-start.8
  80.0 23.8 %copy-start.7 = (f32[1,2048]{1,0:T(1,128)S(1)}, f32[1,2048]{1,0:T(1,128)}, u32[]{:S(2)}) copy-start(f32[1,2048]{1,0:T(1,128)} %param.14) | copy-start | bytes 24580
  107.0 13.7 %collective-permute-start.1 = (bf16[128,2048]{0,1:T(8,128)(2,1)S(1)}, bf16[128,2048]{0,1:T(8,128)(2,1)S(1)}, u32[]{:S(2)}, u32[]{:S(2)}) collective-permute-start(bf16[128,2048]{0,1:T(8,128)(2,1)S(1)} %fusion.25), channel_id=1, source_target_pairs={{0,128},{128,256},{256,384},{384,0},{1,129},{129,257},{257,385},{3... | collective-permute-start | bytes 1572872 | tf_op jit(solution)/shard_map/ppermute | solution.py:46
where the time goes:
time: 123 us; the launch traced here: 122 us
  waiting for transfers between devices  41.1 us (33%)
  starting transfers between devices  37.3 us (30%)
  blocking collectives  25.9 us (21%)
  other arithmetic  8.01 us (7%)
  local copies, waits for them, and re-layouts  7.64 us (6%)
  matrix products  1.94 us (2%)
    all_to_all x1, blocking collectives, local(): conv = lax.all_to_all(conv, 'ctx', split_axis=0, concat_axis=0, tiled=True)  23.4 us
    all_to_all x1, waiting for transfers between devices, local(): lax.all_to_all(signal, 'ctx', split_axis=0, concat_axis=0, tiled=True)  18.4 us
    all_to_all x1, starting transfers between devices, local(): lax.all_to_all(kernel, 'ctx', split_axis=0, concat_axis=0, tiled=True)  16.5 us
    all_to_all x1, starting transfers between devices, local(): lax.all_to_all(signal, 'ctx', split_axis=0, concat_axis=0, tiled=True)  14 us
    ppermute x1, waiting for transfers between devices, from_behind(): return lax.ppermute(block, axis, route)  12.4 us
    ppermute x1, waiting for transfers between devices, passed_along(): return lax.ppermute(x, axis, [(i, (i + by) % peers) for i in range(peers)])  10.3 us
    unnamed x20, local copies, waits for them, and re-layouts  5.5 us
    ppermute x1, starting transfers between devices, passed_along(): return lax.ppermute(x, axis, [(i, (i + by) % peers) for i in range(peers)])  3.41 us
  transfers between devices with their start and end apart: 4, of which 3 were waited for; matrix products, arithmetic and copies ran while one was open for 4% of the time, Pallas kernels for 0%

commit v1 on v0

v1 whole, which is shorter than its diff:
```python
import functools

import jax
import jax.numpy as jnp
import numpy as np
from jax import lax
from jax.experimental import pallas as pl
from jax.experimental.pallas import tpu as pltpu
from jax.sharding import PartitionSpec as P

CHAN = 4096
TAPS = 3
BLOCK = 128
SEQ = 8192
HALF = SEQ // BLOCK
SPAN = 2 * HALF
TOTAL = SPAN * BLOCK
ROWS = HALF + 1
PAD = 80
SIDE = 8
TOGETHER = 4
MESH = pl.DeviceIdType.MESH


def unit_pair(position, period):
    mirror = period - position
    folded = np.minimum(position, mirror)
    angle = folded.astype(np.float32) * np.float32(2 * np.pi / period)
    cosine = np.where(4 * folded == period, 0.0, np.cos(angle)).astype(np.float32)
    sine = np.where((folded == 0) | (2 * folded == period), 0.0, np.sin(angle)).astype(np.float32)
    sine = np.where(position > mirror, -sine, sine)
    return cosine, -sine


def padded(rows):
    return np.pad(rows, ((0, PAD - ROWS), (0, 0)))


def tables():
    k1 = np.arange(ROWS)
    a = np.arange(HALF)
    b = np.arange(BLOCK)
    outer_re, outer_im = unit_pair(k1[:, None] * a[None, :] % SPAN, SPAN)
    inner_re, inner_im = unit_pair(b[:, None] * b[None, :] % BLOCK, BLOCK)
    turn_re, turn_im = unit_pair(k1[:, None] * b[None, :] % TOTAL, TOTAL)
    fold = np.full((ROWS, 1), 2.0 / TOTAL, np.float32)
    fold[0] = fold[-1] = 1.0 / TOTAL
    outer = jnp.asarray(np.concatenate([padded(outer_re), padded(outer_im)]), jnp.bfloat16)
    forward = jnp.asarray(np.block([[inner_re, inner_im], [-inner_im, inner_re]]), jnp.bfloat16)
    inverse = jnp.asarray(np.block([[inner_re, -inner_im], [inner_im, inner_re]]), jnp.bfloat16)
    turn = jnp.asarray(np.stack([padded(turn_re), padded(turn_im)]), jnp.float32)
    rounded = [padded(np.asarray(t.astype(jnp.bfloat16)).astype(np.float32) * fold) for t in (outer_re, outer_im)]
    final = jnp.asarray(np.concatenate(rounded).T, jnp.bfloat16)
    return outer, forward, inverse, turn, final


def from_behind(block, axis, distance):
    devices = range(lax.axis_size(axis))
    route = [(i - distance, i) for i in devices if i - distance in devices]
    return lax.ppermute(block, axis, route)


def passed_along(x, axis, by):
    peers = lax.axis_size(axis)
    return lax.ppermute(x, axis, [(i, (i + by) % peers) for i in range(peers)])


def dot32(left, right):
    return lax.dot_general(left, right, (((1,), (0,)), ((), ())), preferred_element_type=jnp.float32)


def transform(slabs, outer, forward, turn):
    first = dot32(outer[...], jnp.concatenate(slabs, axis=1).astype(jnp.bfloat16))
    turned = []
    for j in range(len(slabs)):
        re = first[:PAD, j * BLOCK : (j + 1) * BLOCK]
        im = first[PAD:, j * BLOCK : (j + 1) * BLOCK]
        turned_re = turn[0] * re - turn[1] * im
        turned_im = turn[0] * im + turn[1] * re
        turned.append(jnp.concatenate([turned_re, turned_im], axis=1).astype(jnp.bfloat16))
    return dot32(jnp.concatenate(turned, axis=0), forward[...])


def untransform(spec, count, filt_re, filt_im, inverse, turn, final):
    weighted = []
    for j in range(count):
        re = spec[j * PAD : (j + 1) * PAD, :BLOCK]
        im = spec[j * PAD : (j + 1) * PAD, BLOCK:]
        out_re = re * filt_re - im * filt_im
        out_im = re * filt_im + im * filt_re
        weighted.append(jnp.concatenate([out_re, out_im], axis=1).astype(jnp.bfloat16))
    back = dot32(jnp.concatenate(weighted, axis=0), inverse[...])
    unturned = []
    for j in range(count):
        re = back[j * PAD : (j + 1) * PAD, :BLOCK]
        im = back[j * PAD : (j + 1) * PAD, BLOCK:]
        out_re = turn[0] * re + turn[1] * im
        out_im = turn[0] * im - turn[1] * re
        unturned.append(jnp.concatenate([out_re, out_im], axis=0).astype(jnp.bfloat16))
    return dot32(final[...], jnp.concatenate(unturned, axis=1))


def middle(
    x_ref, f_ref, outer, forward, inverse, turn, final, o_ref,
    got, got_f, wide, wide_f, filt, result, ready,
    met, send_sem, recv_sem, fsend_sem, frecv_sem, bsend_sem, brecv_sem,
):
    peers = HALF
    chans = x_ref.shape[1]
    filters = f_ref.shape[1]
    me = lax.axis_index("ctx")
    z, y = me // SIDE, me % SIDE
    barrier = pltpu.get_barrier_semaphore()
    for k in range(1, SIDE):
        pl.semaphore_signal(barrier, inc=1, device_id={"ctx": z * SIDE + (y + k) % SIDE}, device_id_type=MESH)
        pl.semaphore_signal(barrier, inc=1, device_id={"ctx": (z + k) % SIDE * SIDE + y}, device_id_type=MESH)
    pl.semaphore_wait(barrier, 2 * (SIDE - 1))
    for k in range(1, SIDE):
        pl.semaphore_signal(met, inc=1, device_id={"ctx": (z + k) % SIDE * SIDE + y}, device_id_type=MESH)
    pl.semaphore_wait(met, SIDE - 1)

    def peer(k):
        kk = (k * 27) % peers
        return (z + kk // SIDE) % SIDE * SIDE + (y + kk % SIDE) % SIDE

    def copy(src, dst, send, recv, k):
        to = peer(k)
        return pltpu.make_async_remote_copy(
            src_ref=src.at[to], dst_ref=dst.at[me], send_sem=send.at[k], recv_sem=recv.at[k],
            device_id={"ctx": to}, device_id_type=MESH,
        )

    def start(k, carry):
        copy(f_ref, got_f, fsend_sem, frecv_sem, k).start()
        copy(x_ref, got, send_sem, recv_sem, k).start()
        return carry

    lax.fori_loop(1, peers, start, 0)
    got[me] = x_ref[me]
    got_f[me] = f_ref[me]

    def wait(src, dst, send, recv):
        def body(k, carry):
            copy(src, dst, send, recv, k).wait()
            return carry

        lax.fori_loop(1, peers, body, 0)

    wait(f_ref, got_f, fsend_sem, frecv_sem)
    wide_f[...] = got_f[...].astype(jnp.float32)
    spec = transform([wide_f[:, f, :] for f in range(filters)], outer, forward, turn)
    for f in range(filters):
        filt[f] = spec[f * PAD : (f + 1) * PAD]
    wait(x_ref, got, send_sem, recv_sem)
    wide[...] = got[...].astype(jnp.float32).reshape(wide.shape)

    def group(g, carry):
        at = [g * TOGETHER + j for j in range(TOGETHER)]
        slabs = [wide[pl.ds(c, peers, stride=chans), :] for c in at]
        spec = transform(slabs, outer, forward, turn)
        gain = filt[g * TOGETHER // (chans // filters)]
        conv = untransform(spec, TOGETHER, gain[:, :BLOCK], gain[:, BLOCK:], inverse, turn, final)
        for j, c in enumerate(at):
            result[pl.ds(c, peers, stride=chans), :] = conv[:, j * BLOCK : (j + 1) * BLOCK]
        return carry

    lax.fori_loop(0, chans // TOGETHER, group, 0)
    ready[...] = result[...].reshape(ready.shape).astype(jnp.bfloat16)

    def start_back(k, carry):
        copy(ready, o_ref, bsend_sem, brecv_sem, k).start()
        return carry

    lax.fori_loop(1, peers, start_back, 0)
    o_ref[me] = ready[me]
    wait(ready, o_ref, bsend_sem, brecv_sem)


def convolve(signal, kernel):
    peers, chans, _ = signal.shape
    filters = kernel.shape[1]
    vmem = pl.BlockSpec(memory_space=pltpu.VMEM)
    sems = pltpu.SemaphoreType.DMA((peers,))
    return pl.pallas_call(
        middle,
        out_shape=jax.ShapeDtypeStruct(signal.shape, jnp.bfloat16),
        in_specs=[vmem] * 7,
        out_specs=vmem,
        scratch_shapes=[
            pltpu.VMEM(signal.shape, jnp.bfloat16),
            pltpu.VMEM(kernel.shape, jnp.bfloat16),
            pltpu.VMEM((peers * chans, BLOCK), jnp.float32),
            pltpu.VMEM(kernel.shape, jnp.float32),
            pltpu.VMEM((filters, PAD, 2 * BLOCK), jnp.float32),
            pltpu.VMEM((peers * chans, BLOCK), jnp.float32),
            pltpu.VMEM(signal.shape, jnp.bfloat16),
            pltpu.SemaphoreType.REGULAR,
        ]
        + [sems] * 6,
        compiler_params=pltpu.CompilerParams(collective_id=0, has_side_effects=True, vmem_limit_bytes=48 << 20),
        name="middle",
    )(signal, kernel, *tables())


def local(section_input, long_filter, short_filter, skip_gain):
    acts_local = section_input[0]
    tok_rows, chan_local = acts_local.shape
    filt_local = long_filter.shape[2]
    n_ctx = lax.axis_size("ctx")
    partial_squares = jnp.sum(acts_local * acts_local, axis=1)
    total_squares = lax.psum(partial_squares, "tp")
    normed = (acts_local * lax.rsqrt(total_squares / CHAN + 1e-06)[:, None]).astype(jnp.bfloat16)
    earlier = from_behind(normed[tok_rows - (TAPS - 1) :], "ctx", 1)
    extended = jnp.concatenate([earlier, normed], axis=0)
    taps_all = short_filter[0].astype(jnp.float32)
    featured = []
    for feature_id in range(3):
        running = jnp.zeros((tok_rows, chan_local), jnp.float32)
        for offset in range(TAPS):
            begin_row = TAPS - 1 - offset
            running = (
                running
                + taps_all[feature_id, offset][None, :] * extended[begin_row : begin_row + tok_rows]
            )
        featured.append(running)
    query = featured[0].astype(jnp.bfloat16)
    product = (featured[1] * featured[2]).astype(jnp.bfloat16)
    signal = product.T.reshape(n_ctx, chan_local // n_ctx, BLOCK)
    kernel = long_filter[0].T.reshape(n_ctx, filt_local // n_ctx, BLOCK)
    conv = convolve(signal, kernel)
    conv_tokens = conv.reshape(chan_local, BLOCK).T
    finished = acts_local + query.astype(jnp.float32) * (
        conv_tokens.astype(jnp.float32) + skip_gain[0][None, :] * product.astype(jnp.float32)
    )
    received = passed_along(finished.astype(jnp.bfloat16), "section", 1).astype(finished.dtype)
    return received[None]


def solution(mesh):
    in_specs = (
        P("section", "ctx", "tp"),
        P("section", "ctx", "tp"),
        P("section", None, None, "tp"),
        P("section", "tp"),
    )
    out_specs = P("section", "ctx", "tp")
    return jax.shard_map(local, mesh=mesh, in_specs=in_specs, out_specs=out_specs, check_vma=False)
```

time: 123 us -> 88.3 us (0.72)
  the two profiles are of different devices: /device:TPU:16 before, /device:TPU:24 now
where the time goes in v1:
time: 88.3 us; the launch traced here: 87.9 us
  Pallas kernels  55.3 us (63%)
  waiting for transfers between devices  12.6 us (14%)
  starting transfers between devices  8.09 us (9%)
  other arithmetic  5.22 us (6%)
  local copies, waits for them, and re-layouts  4.1 us (5%)
  blocking collectives  2.46 us (3%)
    pallas_call x1, Pallas kernels, convolve(): pl.pallas_call(middle, out_shape=jax.ShapeDtypeStruct(signal.shape, jnp.b...  55.3 us
    ppermute x1, waiting for transfers between devices, passed_along(): return lax.ppermute(x, axis, [(i, (i + by) % peers) for i in range(peers)])  12.1 us
    ppermute x1, starting transfers between devices, from_behind(): return lax.ppermute(block, axis, route)  4.7 us
    ppermute x1, starting transfers between devices, passed_along(): return lax.ppermute(x, axis, [(i, (i + by) % peers) for i in range(peers)])  3.4 us
    psum x1, blocking collectives, local(): total_squares = lax.psum(partial_squares, 'tp')  2.46 us
    unnamed x18, local copies, waits for them, and re-layouts  2.1 us
  transfers between devices with their start and end apart: 2, of which 2 were waited for; matrix products, arithmetic and copies ran while one was open for 0% of the time, Pallas kernels for 0%

profile of v1, /device:TPU:24, one launch (start us, length us, event | category | flops | bytes accessed | tf_op | source)
XLA Modules:
  0.0 87.9 jit_solution(13172710075211028578)
XLA Ops:
  0.0 1.5 %fusion.12 = f32[128]{0:T(128)S(1)} fusion(f32[1,128,2048]{2,1,0:T(8,128)} %param.9), kind=kLoop, calls=%fused_computation.24 | loop fusion | flops 524160 | bytes 1049088 | tf_op jit(solution)/shard_map/reduce_sum | solution.py:210
  1.5 2.5 %psum.7 = f32[128]{0:T(128)S(1)} all-reduce(f32[128]{0:T(128)S(1)} %fusion.12), channel_id=1, replica_groups=mesh['section'=4,'ctx'=64,'tp'=2] {'tp'}, use_global_device_ids=true, to_apply=%region_1.0 | all-reduce | flops 128 | bytes 1024 | tf_op jit(solution)/shard_map/psum | solution.py:211
  3.9 0.1 fusion.13
  4.1 4.7 %collective-permute-start = (bf16[2,2048]{1,0:T(2,128)(2,1)S(1)}, bf16[2,2048]{1,0:T(2,128)(2,1)S(1)}, u32[]{:S(2)}, u32[]{:S(2)}) collective-permute-start(bf16[2,2048]{1,0:T(2,128)(2,1)S(1)} %slice.54), channel_id=1, source_target_pairs={{0,2},{2,4},{4,6},{6,8},{8,10},{10,12},{12,14},{14,16},{16,18},{18... | collective-permute-start | bytes 24584 | tf_op jit(solution)/shard_map/ppermute | solution.py:60
  8.8 0.1 fusion.16
  8.9 0.7 copy-done.7
  9.6 0.1 copy.11
  9.7 0.4 collective-permute-done
  10.1 0.6 fusion.15
  10.7 0.0 copy-start
  10.7 0.0 copy-start.1
  10.8 0.0 copy-start.2
  10.8 0.3 copy.10
  11.1 0.6 copy-done
  11.6 0.1 copy-done.1
  11.7 0.0 copy-done.2
  11.8 55.3 %middle.1 = bf16[64,32,128]{2,1,0:T(8,128)(2,1)S(1)} custom-call(bf16[64,32,128]{2,1,0:T(8,128)(2,1)S(1)} %bitcast.42, bf16[64,2,128]{2,1,0:T(2,128)(2,1)S(1)} %bitcast.43, bf16[160,64]{1,0:T(8,128)(2,1)S(1)} %copy-done.3, bf16[256,256]{1,0:T(8,128)(2,1)S(1)} %copy-done.1, bf16[256,256]{1,0:T(8,128)(2,1)S(1)} %copy-done, f32[2,80,128]{2,1,0:T(8,128)S(1)} %copy-done.2, ...), custom_call_target="tpu_custom_call" | custom-call | tf_op jit(solution)/shard_map/middle/pallas_call | solution.py:184
  67.0 1.1 %bitcast_convert_fusion.1 = f32[2048,128]{1,0:T(8,128)} fusion(bf16[64,32,128]{2,1,0:T(8,128)(2,1)S(1)} %middle.1), kind=kLoop, calls=%fused_computation.31 | loop fusion | flops 262144 | bytes 1572864 | tf_op jit(solution)/shard_map/convert_element_type | solution.py:233
  68.1 1.6 %copy.12 = f32[2048,128]{0,1:T(8,128)S(1)} copy(f32[2048,128]{1,0:T(8,128)} %bitcast_convert_fusion.1) | data formatting | bytes 2097152 | tf_op jit(solution)/shard_map/convert_element_type | solution.py:233
  69.7 0.7 copy-done.8
  70.4 0.9 %fusion.11 = bf16[128,2048]{1,0:T(8,128)(2,1)S(1)} fusion(f32[2048,128]{0,1:T(8,128)S(1)} %copy.12, f32[1,128,2048]{2,1,0:T(8,128)S(1)} %copy-done.5, bf16[128,2048]{1,0:T(8,128)(2,1)S(1)} %fusion.13, bf16[2,2048]{1,0:T(2,128)(2,1)S(1)} %collective-permute-done, f32[2048]{0:T(1024)S(1)} %bitcast.60, f32[2048]{0:T(1024)S(1)} %bitcast.57, ...), kind=kLoop, calls=%fused_computation.21 | loop fusion | flops 8912896 | bytes 3235840 | tf_op jit(solution)/shard_map/convert_element_type | solution.py:235
  71.3 3.4 %collective-permute-start.1 = (bf16[128,2048]{1,0:T(8,128)(2,1)S(1)}, bf16[128,2048]{1,0:T(8,128)(2,1)S(1)}, u32[]{:S(2)}, u32[]{:S(2)}) collective-permute-start(bf16[128,2048]{1,0:T(8,128)(2,1)S(1)} %fusion.11), channel_id=1, source_target_pairs={{0,128},{128,256},{256,384},{384,0},{1,129},{129,257},{257,385},{3... | collective-permute-start | bytes 1572872 | tf_op jit(solution)/shard_map/ppermute | solution.py:65
  74.7 12.1 %collective-permute-done.1 = bf16[128,2048]{1,0:T(8,128)(2,1)S(1)} collective-permute-done((bf16[128,2048]{1,0:T(8,128)(2,1)S(1)}, bf16[128,2048]{1,0:T(8,128)(2,1)S(1)}, u32[]{:S(2)}, u32[]{:S(2)}) %collective-permute-start.1) | collective-permute-done | bytes 524320 | tf_op jit(solution)/shard_map/ppermute | solution.py:65
  86.8 1.1 %bitcast_convert_fusion = f32[1,128,2048]{2,1,0:T(8,128)} fusion(bf16[128,2048]{1,0:T(8,128)(2,1)S(1)} %collective-permute-done.1), kind=kLoop, calls=%fused_computation.30 | loop fusion | flops 262144 | bytes 1572864 | tf_op jit(solution)/shard_map/broadcast_in_dim | solution.py:236
  (13 shorter events, 0.1 us)
Async XLA Ops:
  0.0 3.9 %copy-start.5 = (f32[1,128,2048]{2,1,0:T(8,128)S(1)}, f32[1,128,2048]{2,1,0:T(8,128)}, u32[]{:S(2)}) copy-start(f32[1,128,2048]{2,1,0:T(8,128)} %param.9) | copy-start | bytes 3145732
  3.9 4.9 %copy-start.6 = (bf16[1,3,3,2048]{3,2,1,0:T(4,128)(2,1)S(1)}, bf16[1,3,3,2048]{3,2,1,0:T(4,128)(2,1)}, u32[]{:S(2)}) copy-start(bf16[1,3,3,2048]{3,2,1,0:T(4,128)(2,1)} %param.11) | copy-start | bytes 110596
  4.1 6.0 %collective-permute-start = (bf16[2,2048]{1,0:T(2,128)(2,1)S(1)}, bf16[2,2048]{1,0:T(2,128)(2,1)S(1)}, u32[]{:S(2)}, u32[]{:S(2)}) collective-permute-start(bf16[2,2048]{1,0:T(2,128)(2,1)S(1)} %slice.54), channel_id=1, source_target_pairs={{0,2},{2,4},{4,6},{6,8},{8,10},{10,12},{12,14},{14,16},{16,18},{18... | collective-permute-start | bytes 24584 | tf_op jit(solution)/shard_map/ppermute | solution.py:60
  8.8 0.8 copy-start.7
  10.7 0.9 %copy-start = (bf16[256,256]{1,0:T(8,128)(2,1)S(1)}, bf16[256,256]{1,0:T(8,128)(2,1)}, u32[]{:S(2)}) copy-start(bf16[256,256]{1,0:T(8,128)(2,1)} %constant.19.clone.inverse) | copy-start | bytes 393220
  10.7 1.0 %copy-start.1 = (bf16[256,256]{1,0:T(8,128)(2,1)S(1)}, bf16[256,256]{1,0:T(8,128)(2,1)}, u32[]{:S(2)}) copy-start(bf16[256,256]{1,0:T(8,128)(2,1)} %constant.18.clone.forward) | copy-start | bytes 393220
  10.8 1.0 %copy-start.2 = (f32[2,80,128]{2,1,0:T(8,128)S(1)}, f32[2,80,128]{2,1,0:T(8,128)}, u32[]{:S(2)}) copy-start(f32[2,80,128]{2,1,0:T(8,128)} %constant.20.clone.turn) | copy-start | bytes 245764
  10.8 1.0 %copy-start.3 = (bf16[160,64]{1,0:T(8,128)(2,1)S(1)}, bf16[160,64]{1,0:T(8,128)(2,1)}, u32[]{:S(2)}) copy-start(bf16[160,64]{1,0:T(8,128)(2,1)} %constant.17.clone.outer) | copy-start | bytes 61444
  10.8 1.0 %copy-start.4 = (bf16[64,160]{1,0:T(8,128)(2,1)S(1)}, bf16[64,160]{1,0:T(8,128)(2,1)}, u32[]{:S(2)}) copy-start(bf16[64,160]{1,0:T(8,128)(2,1)} %constant.21.clone.final) | copy-start | bytes 61444
  69.7 0.7 copy-start.8
  71.3 15.5 %collective-permute-start.1 = (bf16[128,2048]{1,0:T(8,128)(2,1)S(1)}, bf16[128,2048]{1,0:T(8,128)(2,1)S(1)}, u32[]{:S(2)}, u32[]{:S(2)}) collective-permute-start(bf16[128,2048]{1,0:T(8,128)(2,1)S(1)} %fusion.11), channel_id=1, source_target_pairs={{0,128},{128,256},{256,384},{384,0},{1,129},{129,257},{257,385},{3... | collective-permute-start | bytes 1572872 | tf_op jit(solution)/shard_map/ppermute | solution.py:65

commit v2 on v1

v2 whole, which is shorter than its diff:
```python
import functools

import jax
import jax.numpy as jnp
import numpy as np
from jax import lax
from jax.experimental import pallas as pl
from jax.experimental.pallas import tpu as pltpu
from jax.sharding import PartitionSpec as P

CHAN = 4096
TAPS = 3
BLOCK = 128
SEQ = 8192
HALF = SEQ // BLOCK
SPAN = 2 * HALF
TOTAL = SPAN * BLOCK
ROWS = HALF + 1
PAD = 80
SIDE = 8
TOGETHER = 4
GROUP = 16
HALVES = 2
HALO = 2
TOP = 8
MESH = pl.DeviceIdType.MESH


def unit_pair(position, period):
    mirror = period - position
    folded = np.minimum(position, mirror)
    angle = folded.astype(np.float32) * np.float32(2 * np.pi / period)
    cosine = np.where(4 * folded == period, 0.0, np.cos(angle)).astype(np.float32)
    sine = np.where((folded == 0) | (2 * folded == period), 0.0, np.sin(angle)).astype(np.float32)
    sine = np.where(position > mirror, -sine, sine)
    return cosine, -sine


def padded(rows):
    return np.pad(rows, ((0, PAD - ROWS), (0, 0)))


def tables():
    k1 = np.arange(ROWS)
    a = np.arange(HALF)
    b = np.arange(BLOCK)
    outer_re, outer_im = unit_pair(k1[:, None] * a[None, :] % SPAN, SPAN)
    inner_re, inner_im = unit_pair(b[:, None] * b[None, :] % BLOCK, BLOCK)
    turn_re, turn_im = unit_pair(k1[:, None] * b[None, :] % TOTAL, TOTAL)
    fold = np.full((ROWS, 1), 2.0 / TOTAL, np.float32)
    fold[0] = fold[-1] = 1.0 / TOTAL
    outer = jnp.asarray(np.concatenate([padded(outer_re), padded(outer_im)]), jnp.bfloat16)
    forward = jnp.asarray(np.block([[inner_re, inner_im], [-inner_im, inner_re]]), jnp.bfloat16)
    inverse = jnp.asarray(np.block([[inner_re, -inner_im], [inner_im, inner_re]]), jnp.bfloat16)
    turn = jnp.asarray(np.stack([padded(turn_re), padded(turn_im)]), jnp.float32)
    rounded = [padded(np.asarray(t.astype(jnp.bfloat16)).astype(np.float32) * fold) for t in (outer_re, outer_im)]
    final = jnp.asarray(np.concatenate(rounded).T, jnp.bfloat16)
    return outer, forward, inverse, turn, final


def dot32(left, right):
    return lax.dot_general(left, right, (((1,), (0,)), ((), ())), preferred_element_type=jnp.float32)


def transform(slabs, outer, forward, turn):
    first = dot32(outer[...], jnp.concatenate(slabs, axis=1).astype(jnp.bfloat16))
    turned = []
    for j in range(len(slabs)):
        re = first[:PAD, j * BLOCK : (j + 1) * BLOCK]
        im = first[PAD:, j * BLOCK : (j + 1) * BLOCK]
        turned_re = turn[0] * re - turn[1] * im
        turned_im = turn[0] * im + turn[1] * re
        turned.append(jnp.concatenate([turned_re, turned_im], axis=1).astype(jnp.bfloat16))
    return dot32(jnp.concatenate(turned, axis=0), forward[...])


def untransform(spec, count, filt_re, filt_im, inverse, turn, final):
    weighted = []
    for j in range(count):
        re = spec[j * PAD : (j + 1) * PAD, :BLOCK]
        im = spec[j * PAD : (j + 1) * PAD, BLOCK:]
        out_re = re * filt_re - im * filt_im
        out_im = re * filt_im + im * filt_re
        weighted.append(jnp.concatenate([out_re, out_im], axis=1).astype(jnp.bfloat16))
    back = dot32(jnp.concatenate(weighted, axis=0), inverse[...])
    unturned = []
    for j in range(count):
        re = back[j * PAD : (j + 1) * PAD, :BLOCK]
        im = back[j * PAD : (j + 1) * PAD, BLOCK:]
        out_re = turn[0] * re + turn[1] * im
        out_im = turn[0] * im - turn[1] * re
        unturned.append(jnp.concatenate([out_re, out_im], axis=0).astype(jnp.bfloat16))
    return dot32(final[...], jnp.concatenate(unturned, axis=1))


def tick(
    x_hbm, filter_hbm, short_hbm, skip_hbm, outer_hbm, forward_hbm, inverse_hbm, turn_hbm, final_hbm, o_ref,
    x, kern, short, skip, outer, forward, inverse, turn, final,
    edge, halo, squares, other_squares, taps, normed, query, kern_out, kern_in, kern_wide, filt,
    product, got, wide, result, ready, conv, finished,
    met, load_sem, edge_send, edge_recv, sq_send, sq_recv, kern_send, kern_recv,
    prod_send, prod_recv, conv_send, conv_recv, hop_send, hop_recv,
):
    rows, chans = x.shape
    half_chans = chans // HALVES
    section, ctx, tp = lax.axis_index("section"), lax.axis_index("ctx"), lax.axis_index("tp")
    n_section = lax.axis_size("section")
    z, y = ctx // SIDE, ctx % SIDE
    following, before = (ctx + 1) % HALF, (ctx + HALF - 1) % HALF

    pairs = (
        (x_hbm, x), (filter_hbm, kern), (short_hbm, short), (skip_hbm, skip), (outer_hbm, outer),
        (forward_hbm, forward), (inverse_hbm, inverse), (turn_hbm, turn), (final_hbm, final),
    )
    loads = [pltpu.make_async_copy(src, dst, load_sem.at[i]) for i, (src, dst) in enumerate(pairs)]
    for load in loads:
        load.start()

    barrier = pltpu.get_barrier_semaphore()

    def greet(sem, **to):
        pl.semaphore_signal(sem, inc=1, device_id=to, device_id_type=MESH)

    greet(barrier, tp=1 - tp)
    greet(barrier, ctx=before, tp=0)
    greet(barrier, ctx=before, tp=1)
    for k in range(1, SIDE):
        greet(barrier, ctx=(z + k) % SIDE * SIDE + y)
        greet(barrier, ctx=z * SIDE + (y + k) % SIDE)
    greet(barrier, section=(section + n_section - 1) % n_section)

    loads[0].wait()
    edge[...] = x[rows - HALO :, :]
    total = jnp.zeros((rows, BLOCK), jnp.float32)
    for j in range(chans // BLOCK):
        part = x[:, j * BLOCK : (j + 1) * BLOCK]
        total = total + part * part
    squares[...] = total
    pl.semaphore_wait(barrier, 2 * (SIDE - 1) + 4)
    for k in range(1, SIDE):
        greet(met, ctx=(z + k) % SIDE * SIDE + y)

    def remote(src, dst, send, recv, **to):
        return pltpu.make_async_remote_copy(
            src_ref=src, dst_ref=dst, send_sem=send, recv_sem=recv, device_id=to, device_id_type=MESH
        )

    swap = remote(squares, other_squares, sq_send, sq_recv, tp=1 - tp)
    swap.start()
    edges = [
        remote(edge, halo.at[0], edge_send.at[0], edge_recv.at[0], ctx=following),
        remote(edge, halo.at[1], edge_send.at[1], edge_recv.at[1], ctx=following, tp=1 - tp),
    ]
    for send in edges:
        send.start()

    for load in loads[1:]:
        load.wait()
    kern_rows = kern[...].astype(jnp.float32).T
    for h in range(HALVES):
        kern_out[:, h, :] = kern_rows[h * HALF : (h + 1) * HALF]
    for f in range(3):
        taps[f] = short[f].astype(jnp.float32)
    pl.semaphore_wait(met, SIDE - 1)

    def at(dz, dy):
        return (z + dz) % SIDE * SIDE + (y + dy) % SIDE

    def send_kern(k, carry):
        to = at(k // SIDE, k % SIDE)
        remote(kern_out.at[to], kern_in.at[ctx], kern_send, kern_recv, ctx=to).start()
        return carry

    lax.fori_loop(1, HALF, send_kern, 0)
    pltpu.make_async_copy(kern_out.at[ctx], kern_in.at[ctx], kern_recv).start()

    swap.wait()
    mean = jnp.sum(squares[...] + other_squares[...], axis=1, keepdims=True) / CHAN
    scale = lax.rsqrt(mean + 1e-06)
    for j in range(chans // BLOCK):
        lanes = slice(j * BLOCK, (j + 1) * BLOCK)
        normed[TOP:, lanes] = (x[:, lanes] * scale).astype(jnp.bfloat16).astype(jnp.float32)
    for send in edges:
        send.wait()
    mine, theirs = halo[0], halo[1]
    edge_mean = (
        jnp.sum(mine * mine, axis=1, keepdims=True) + jnp.sum(theirs * theirs, axis=1, keepdims=True)
    ) / CHAN
    edge_normed = (mine * lax.rsqrt(edge_mean + 1e-06)).astype(jnp.bfloat16).astype(jnp.float32)
    normed[TOP - HALO : TOP, :] = jnp.where(ctx == 0, 0.0, edge_normed)

    for h in range(HALVES):

        def chunk(i, carry):
            dz = i * 3 % SIDE
            row = (z + dz) % SIDE
            lanes = pl.ds(pl.multiple_of(h * half_chans + row * BLOCK, BLOCK), BLOCK)
            shifted = [normed[pl.ds(TOP - t, rows), lanes] for t in range(TAPS)]
            features = []
            for f in range(3):
                running = taps[f, pl.ds(0, 1), lanes] * shifted[0]
                for t in range(1, TAPS):
                    running = running + taps[f, pl.ds(t, 1), lanes] * shifted[t]
                features.append(running)
            ask = features[0].astype(jnp.bfloat16).astype(jnp.float32)
            gated = (features[1] * features[2]).astype(jnp.bfloat16).astype(jnp.float32)
            query[:, lanes] = ask
            x[:, lanes] = x[:, lanes] + ask * (skip[:, lanes] * gated)
            product[h, pl.ds(row * SIDE, SIDE)] = gated.T.astype(jnp.bfloat16).reshape(SIDE, GROUP, BLOCK)

            def send(r, inner):
                to = row * SIDE + (y + r) % SIDE
                remote(product.at[h, to], got.at[h, ctx], prod_send.at[h], prod_recv.at[h], ctx=to).start()
                return inner

            lax.fori_loop(jnp.where(i == 0, 1, 0), SIDE, send, 0)
            return carry

        lax.fori_loop(0, SIDE, chunk, 0)
        pltpu.make_async_copy(product.at[h, ctx], got.at[h, ctx], prod_recv.at[h]).start()

    def wait_in(dst, sem):
        pltpu.make_async_copy(dst, dst, sem).wait()

    wait_in(kern_in, kern_recv)
    kern_wide[...] = kern_in[...]
    spec = transform([kern_wide[:, h, :] for h in range(HALVES)], outer, forward, turn)
    for h in range(HALVES):
        filt[h] = spec[h * PAD : (h + 1) * PAD]

    for h in range(HALVES):
        wait_in(got.at[h], prod_recv.at[h])
        wide[...] = got[h].astype(jnp.float32).reshape(wide.shape)

        def group(g, carry):
            ids = [g * TOGETHER + j for j in range(TOGETHER)]
            slabs = [wide[pl.ds(c, HALF, stride=GROUP), :] for c in ids]
            spec = transform(slabs, outer, forward, turn)
            gain = filt[h]
            out = untransform(spec, TOGETHER, gain[:, :BLOCK], gain[:, BLOCK:], inverse, turn, final)
            for j, c in enumerate(ids):
                result[pl.ds(c, HALF, stride=GROUP), :] = out[:, j * BLOCK : (j + 1) * BLOCK]
            return carry

        lax.fori_loop(0, GROUP // TOGETHER, group, 0)
        ready[h] = result[...].reshape(HALF, GROUP, BLOCK).astype(jnp.bfloat16)

        def send_back(k, carry):
            to = at(k // SIDE * 3 % SIDE, k % SIDE)
            remote(ready.at[h, to], conv.at[h, ctx], conv_send.at[h], conv_recv.at[h, z], ctx=to).start()
            return carry

        lax.fori_loop(1, HALF, send_back, 0)
        pltpu.make_async_copy(ready.at[h, ctx], conv.at[h, ctx], conv_recv.at[h, z]).start()

    onward = (section + 1) % n_section
    for h in range(HALVES):

        def finish(i, carry):
            row = (z + SIDE - i * 3 % SIDE) % SIDE
            blocks = pl.ds(row * SIDE, SIDE)
            lanes = pl.ds(pl.multiple_of(h * half_chans + row * BLOCK, BLOCK), BLOCK)
            wait_in(conv.at[h, blocks], conv_recv.at[h, row])
            got_conv = conv[h, blocks].astype(jnp.float32).reshape(BLOCK, BLOCK).T
            finished[:, lanes] = (x[:, lanes] + query[:, lanes] * got_conv).astype(jnp.bfloat16)
            remote(finished.at[:, lanes], o_ref.at[:, lanes], hop_send, hop_recv, section=onward).start()
            return carry

        lax.fori_loop(0, SIDE, finish, 0)

    remote(finished, o_ref, hop_send, hop_recv, section=onward).wait()
    sent = pl.ds(0, HALF - 1)
    pltpu.make_async_copy(kern_out.at[sent], kern_out.at[sent], kern_send).wait()
    for h in range(HALVES):
        wait_in(product.at[h, sent], prod_send.at[h])
        wait_in(ready.at[h, sent], conv_send.at[h])


def local(section_input, long_filter, short_filter, skip_gain):
    rows, chans = section_input.shape[1:]
    args = (section_input[0], long_filter[0], short_filter[0], skip_gain, *tables())
    anywhere = pl.BlockSpec(memory_space=pl.ANY)
    half_blocks = (HALVES, HALF, GROUP, BLOCK)
    f32, bf16 = jnp.float32, jnp.bfloat16
    dma = pltpu.SemaphoreType.DMA
    scratch = [pltpu.VMEM(arg.shape, arg.dtype) for arg in args] + [
        pltpu.VMEM((HALO, chans), f32),
        pltpu.VMEM((2, HALO, chans), f32),
        pltpu.VMEM((rows, BLOCK), f32),
        pltpu.VMEM((rows, BLOCK), f32),
        pltpu.VMEM((3, TAPS, chans), f32),
        pltpu.VMEM((TOP + rows, chans), f32),
        pltpu.VMEM((rows, chans), f32),
        pltpu.VMEM((HALF, HALVES, BLOCK), f32),
        pltpu.VMEM((HALF, HALVES, BLOCK), f32),
        pltpu.VMEM((HALF, HALVES, BLOCK), f32),
        pltpu.VMEM((HALVES, PAD, 2 * BLOCK), f32),
        pltpu.VMEM(half_blocks, bf16),
        pltpu.VMEM(half_blocks, bf16),
        pltpu.VMEM((HALF * GROUP, BLOCK), f32),
        pltpu.VMEM((HALF * GROUP, BLOCK), f32),
        pltpu.VMEM(half_blocks, bf16),
        pltpu.VMEM(half_blocks, bf16),
        pltpu.VMEM((rows, chans), bf16),
        pltpu.SemaphoreType.REGULAR,
        dma((len(args),)),
        dma((2,)), dma((2,)),
        dma, dma,
        dma, dma,
        dma((HALVES,)), dma((HALVES,)),
        dma((HALVES,)), dma((HALVES, SIDE)),
        dma, dma,
    ]
    received = pl.pallas_call(
        tick,
        out_shape=jax.ShapeDtypeStruct((rows, chans), bf16),
        in_specs=[anywhere] * len(args),
        out_specs=pl.BlockSpec(memory_space=pltpu.VMEM),
        scratch_shapes=scratch,
        compiler_params=pltpu.CompilerParams(collective_id=0, has_side_effects=True, vmem_limit_bytes=48 << 20),
        name="tick",
    )(*args)
    return received.astype(section_input.dtype)[None]


def solution(mesh):
    in_specs = (
        P("section", "ctx", "tp"),
        P("section", "ctx", "tp"),
        P("section", None, None, "tp"),
        P("section", "tp"),
    )
    out_specs = P("section", "ctx", "tp")
    return jax.shard_map(local, mesh=mesh, in_specs=in_specs, out_specs=out_specs, check_vma=False)
```

time: 88.3 us -> 63 us (0.71)
  the two profiles are of different devices: /device:TPU:24 before, /device:TPU:1 now
where the time goes in v2:
time: 63 us; the launch traced here: 62.5 us
  Pallas kernels  53.7 us (85%)
  local copies, waits for them, and re-layouts  7.7 us (12%)
  other arithmetic  1.07 us (2%)
    pallas_call x1, Pallas kernels, local(): pl.pallas_call(tick, out_shape=jax.ShapeDtypeStruct((rows, chans), bf16),...  53.7 us
    unnamed x18, local copies, waits for them, and re-layouts  7.7 us

profile of v2, /device:TPU:1, one launch (start us, length us, event | category | flops | bytes accessed | tf_op | source)
XLA Modules:
  0.0 62.5 jit_solution(1882768935898706817)
XLA Ops:
  0.0 0.0 copy-start
  0.0 1.2 %copy-done = f32[1,128,2048]{2,1,0:T(8,128)S(1)} copy-done((f32[1,128,2048]{2,1,0:T(8,128)S(1)}, f32[1,128,2048]{2,1,0:T(8,128)}, u32[]{:S(2)}) %copy-start) | copy-done | bytes 1048600
  1.2 0.0 copy-start.1
  1.2 0.9 %copy-done.1 = bf16[256,256]{1,0:T(8,128)(2,1)S(1)} copy-done((bf16[256,256]{1,0:T(8,128)(2,1)S(1)}, bf16[256,256]{1,0:T(8,128)(2,1)}, u32[]{:S(2)}) %copy-start.1) | copy-done | bytes 131096
  2.1 0.0 copy-start.2
  2.1 0.9 %copy-done.2 = bf16[256,256]{1,0:T(8,128)(2,1)S(1)} copy-done((bf16[256,256]{1,0:T(8,128)(2,1)S(1)}, bf16[256,256]{1,0:T(8,128)(2,1)}, u32[]{:S(2)}) %copy-start.2) | copy-done | bytes 131096
  3.0 0.0 copy-start.3
  3.0 0.9 %copy-done.3 = f32[2,80,128]{2,1,0:T(8,128)S(1)} copy-done((f32[2,80,128]{2,1,0:T(8,128)S(1)}, f32[2,80,128]{2,1,0:T(8,128)}, u32[]{:S(2)}) %copy-start.3) | copy-done | bytes 81944
  3.9 0.0 copy-start.4
  3.9 0.8 %copy-done.4 = bf16[1,3,3,2048]{3,2,1,0:T(4,128)(2,1)S(1)} copy-done((bf16[1,3,3,2048]{3,2,1,0:T(4,128)(2,1)S(1)}, bf16[1,3,3,2048]{3,2,1,0:T(4,128)(2,1)}, u32[]{:S(2)}) %copy-start.4) | copy-done | bytes 36888
  4.7 0.0 copy-start.5
  4.7 0.8 %copy-done.5 = bf16[160,64]{1,0:T(8,128)(2,1)S(1)} copy-done((bf16[160,64]{1,0:T(8,128)(2,1)S(1)}, bf16[160,64]{1,0:T(8,128)(2,1)}, u32[]{:S(2)}) %copy-start.5) | copy-done | bytes 20504
  5.5 0.0 copy-start.6
  5.5 0.8 %copy-done.6 = bf16[1,128,128]{2,1,0:T(8,128)(2,1)S(1)} copy-done((bf16[1,128,128]{2,1,0:T(8,128)(2,1)S(1)}, bf16[1,128,128]{2,1,0:T(8,128)(2,1)}, u32[]{:S(2)}) %copy-start.6) | copy-done | bytes 32792
  6.3 0.0 copy-start.7
  6.3 0.8 %copy-done.7 = bf16[64,160]{1,0:T(8,128)(2,1)S(1)} copy-done((bf16[64,160]{1,0:T(8,128)(2,1)S(1)}, bf16[64,160]{1,0:T(8,128)(2,1)}, u32[]{:S(2)}) %copy-start.7) | copy-done | bytes 20504
  7.0 0.0 copy-start.8
  7.0 0.7 %copy-done.8 = f32[1,2048]{1,0:T(1,128)S(1)} copy-done((f32[1,2048]{1,0:T(1,128)S(1)}, f32[1,2048]{1,0:T(1,128)}, u32[]{:S(2)}) %copy-start.8) | copy-done | bytes 8216
  7.7 53.7 %tick.1 = bf16[128,2048]{1,0:T(8,128)(2,1)S(1)} custom-call(f32[128,2048]{1,0:T(8,128)S(1)} %bitcast.6, bf16[128,128]{1,0:T(8,128)(2,1)S(1)} %bitcast.8, bf16[3,3,2048]{2,1,0:T(4,128)(2,1)S(1)} %bitcast.7, f32[1,2048]{1,0:T(1,128)S(1)} %copy-done.8, bf16[160,64]{1,0:T(8,128)(2,1)S(1)} %copy-done.5, bf16[256,256]{1,0:T(8,128)(2,1)S(1)} %copy-done.2, ...), custom_call_target="tpu_custom_call" | custom-call | tf_op jit(solution)/shard_map/tick/pallas_call | solution.py:314
  61.4 1.1 %bitcast_convert_fusion = f32[1,128,2048]{2,1,0:T(8,128)} fusion(bf16[128,2048]{1,0:T(8,128)(2,1)S(1)} %tick.1), kind=kLoop, calls=%fused_computation | loop fusion | flops 262144 | bytes 1572864 | tf_op jit(solution)/shard_map/broadcast_in_dim | solution.py:323
Async XLA Ops:
  0.0 1.2 %copy-start = (f32[1,128,2048]{2,1,0:T(8,128)S(1)}, f32[1,128,2048]{2,1,0:T(8,128)}, u32[]{:S(2)}) copy-start(f32[1,128,2048]{2,1,0:T(8,128)} %param.9) | copy-start | bytes 3145732
  1.2 0.9 %copy-start.1 = (bf16[256,256]{1,0:T(8,128)(2,1)S(1)}, bf16[256,256]{1,0:T(8,128)(2,1)}, u32[]{:S(2)}) copy-start(bf16[256,256]{1,0:T(8,128)(2,1)} %constant.12.clone.inverse_hbm) | copy-start | bytes 393220
  2.1 0.9 %copy-start.2 = (bf16[256,256]{1,0:T(8,128)(2,1)S(1)}, bf16[256,256]{1,0:T(8,128)(2,1)}, u32[]{:S(2)}) copy-start(bf16[256,256]{1,0:T(8,128)(2,1)} %constant.11.clone.forward_hbm) | copy-start | bytes 393220
  3.0 0.9 %copy-start.3 = (f32[2,80,128]{2,1,0:T(8,128)S(1)}, f32[2,80,128]{2,1,0:T(8,128)}, u32[]{:S(2)}) copy-start(f32[2,80,128]{2,1,0:T(8,128)} %constant.13.clone.turn_hbm) | copy-start | bytes 245764
  3.9 0.8 %copy-start.4 = (bf16[1,3,3,2048]{3,2,1,0:T(4,128)(2,1)S(1)}, bf16[1,3,3,2048]{3,2,1,0:T(4,128)(2,1)}, u32[]{:S(2)}) copy-start(bf16[1,3,3,2048]{3,2,1,0:T(4,128)(2,1)} %param.11) | copy-start | bytes 110596
  4.7 0.8 %copy-start.5 = (bf16[160,64]{1,0:T(8,128)(2,1)S(1)}, bf16[160,64]{1,0:T(8,128)(2,1)}, u32[]{:S(2)}) copy-start(bf16[160,64]{1,0:T(8,128)(2,1)} %constant.10.clone.outer_hbm) | copy-start | bytes 61444
  5.5 0.8 %copy-start.6 = (bf16[1,128,128]{2,1,0:T(8,128)(2,1)S(1)}, bf16[1,128,128]{2,1,0:T(8,128)(2,1)}, u32[]{:S(2)}) copy-start(bf16[1,128,128]{2,1,0:T(8,128)(2,1)} %param.10) | copy-start | bytes 98308
  6.3 0.8 %copy-start.7 = (bf16[64,160]{1,0:T(8,128)(2,1)S(1)}, bf16[64,160]{1,0:T(8,128)(2,1)}, u32[]{:S(2)}) copy-start(bf16[64,160]{1,0:T(8,128)(2,1)} %constant.14.clone.final_hbm) | copy-start | bytes 61444
  7.0 0.7 %copy-start.8 = (f32[1,2048]{1,0:T(1,128)S(1)}, f32[1,2048]{1,0:T(1,128)}, u32[]{:S(2)}) copy-start(f32[1,2048]{1,0:T(1,128)} %skip_hbm.1) | copy-start | bytes 24580

commit v3 on v2

--- a/solution.py
+++ b/solution.py
@@ -317,7 +317,7 @@
         in_specs=[anywhere] * len(args),
         out_specs=pl.BlockSpec(memory_space=pltpu.VMEM),
         scratch_shapes=scratch,
-        compiler_params=pltpu.CompilerParams(collective_id=0, has_side_effects=True, vmem_limit_bytes=48 << 20),
+        compiler_params=pltpu.CompilerParams(collective_id=0, has_side_effects=True, vmem_limit_bytes=56 << 20),
         name="tick",
     )(*args)
     return received.astype(section_input.dtype)[None]

time: 63 us -> 56.1 us (0.89)
  local copies, waits for them, and re-layouts: 7.7 us -> 0 us
  other arithmetic: 1.07 us -> 2.12 us
    unnamed x18 -> x0, local copies, waits for them, and re-layouts: 7.7 us -> none
    broadcast_in_dim x1, other arithmetic: 1.07 us -> 2.12 us  [local(): return received.astype(section_input.dtype)[None]]
where the time goes in v3:
time: 56.1 us; the launch traced here: 56 us
  Pallas kernels  53.8 us (96%)
  other arithmetic  2.12 us (4%)
    pallas_call x1, Pallas kernels, local(): pl.pallas_call(tick, out_shape=jax.ShapeDtypeStruct((rows, chans), bf16),...  53.8 us
    broadcast_in_dim x1, other arithmetic, local(): return received.astype(section_input.dtype)[None]  2.12 us

profile of v3, /device:TPU:1, one launch (start us, length us, event | category | flops | bytes accessed | tf_op | source)
XLA Modules:
  0.0 56.0 jit_solution(18106151795714901266)
XLA Ops:
  0.0 53.8 %tick.1 = bf16[128,2048]{1,0:T(8,128)(2,1)} custom-call(f32[128,2048]{1,0:T(8,128)} %bitcast.6, bf16[128,128]{1,0:T(8,128)(2,1)} %bitcast.8, bf16[3,3,2048]{2,1,0:T(4,128)(2,1)} %bitcast.7, f32[1,2048]{1,0:T(1,128)} %skip_hbm.1, bf16[160,64]{1,0:T(8,128)(2,1)} %constant.10.clone.outer_hbm, bf16[256,256]{1,0:T(8,128)(2,1)} %constant.11.clone.forward_hbm, ...), custom_call_target="tpu_custom_call" | custom-call | tf_op jit(solution)/shard_map/tick/pallas_call | solution.py:314
  53.8 2.1 %bitcast_convert_fusion = f32[1,128,2048]{2,1,0:T(8,128)} fusion(bf16[128,2048]{1,0:T(8,128)(2,1)} %tick.1), kind=kLoop, calls=%fused_computation | loop fusion | flops 262144 | bytes 1572864 | tf_op jit(solution)/shard_map/broadcast_in_dim | solution.py:323

commit v4 on v3

v4 whole, which is shorter than its diff:
```python
import functools

import jax
import jax.numpy as jnp
import numpy as np
from jax import lax
from jax.experimental import pallas as pl
from jax.experimental.pallas import tpu as pltpu
from jax.sharding import PartitionSpec as P

CHAN = 4096
TAPS = 3
BLOCK = 128
SEQ = 8192
HALF = SEQ // BLOCK
SPAN = 2 * HALF
TOTAL = SPAN * BLOCK
ROWS = HALF + 1
PAD = 80
SIDE = 8
TOGETHER = 8
GROUP = 16
HALVES = 2
HALO = 2
TOP = 16
MESH = pl.DeviceIdType.MESH


def unit_pair(position, period):
    mirror = period - position
    folded = np.minimum(position, mirror)
    angle = folded.astype(np.float32) * np.float32(2 * np.pi / period)
    cosine = np.where(4 * folded == period, 0.0, np.cos(angle)).astype(np.float32)
    sine = np.where((folded == 0) | (2 * folded == period), 0.0, np.sin(angle)).astype(np.float32)
    sine = np.where(position > mirror, -sine, sine)
    return cosine, -sine


def padded(rows):
    return np.pad(rows, ((0, PAD - ROWS), (0, 0)))


def tables():
    k1 = np.arange(ROWS)
    a = np.arange(HALF)
    b = np.arange(BLOCK)
    outer_re, outer_im = unit_pair(k1[:, None] * a[None, :] % SPAN, SPAN)
    inner_re, inner_im = unit_pair(b[:, None] * b[None, :] % BLOCK, BLOCK)
    turn_re, turn_im = unit_pair(k1[:, None] * b[None, :] % TOTAL, TOTAL)
    fold = np.full((ROWS, 1), 2.0 / TOTAL, np.float32)
    fold[0] = fold[-1] = 1.0 / TOTAL
    outer = jnp.asarray(np.concatenate([padded(outer_re), padded(outer_im)]), jnp.bfloat16)
    forward = jnp.asarray(np.block([[inner_re, inner_im], [-inner_im, inner_re]]), jnp.bfloat16)
    inverse = jnp.asarray(np.block([[inner_re, -inner_im], [inner_im, inner_re]]), jnp.bfloat16)
    turn = jnp.asarray(np.stack([padded(turn_re), padded(turn_im)]), jnp.float32)
    rounded = [padded(np.asarray(t.astype(jnp.bfloat16)).astype(np.float32) * fold) for t in (outer_re, outer_im)]
    final = jnp.asarray(np.concatenate(rounded).T, jnp.bfloat16)
    return outer, forward, inverse, turn, final


def dot32(left, right):
    return lax.dot_general(left, right, (((1,), (0,)), ((), ())), preferred_element_type=jnp.float32)


def transform(slabs, outer, forward, turn):
    first = dot32(outer[...], jnp.concatenate(slabs, axis=1).astype(jnp.bfloat16))
    turned = []
    for j in range(len(slabs)):
        re = first[:PAD, j * BLOCK : (j + 1) * BLOCK]
        im = first[PAD:, j * BLOCK : (j + 1) * BLOCK]
        turned_re = turn[0] * re - turn[1] * im
        turned_im = turn[0] * im + turn[1] * re
        turned.append(jnp.concatenate([turned_re, turned_im], axis=1).astype(jnp.bfloat16))
    return dot32(jnp.concatenate(turned, axis=0), forward[...])


def untransform(spec, count, filt_re, filt_im, inverse, turn, final):
    weighted = []
    for j in range(count):
        re = spec[j * PAD : (j + 1) * PAD, :BLOCK]
        im = spec[j * PAD : (j + 1) * PAD, BLOCK:]
        out_re = re * filt_re - im * filt_im
        out_im = re * filt_im + im * filt_re
        weighted.append(jnp.concatenate([out_re, out_im], axis=1).astype(jnp.bfloat16))
    back = dot32(jnp.concatenate(weighted, axis=0), inverse[...])
    unturned = []
    for j in range(count):
        re = back[j * PAD : (j + 1) * PAD, :BLOCK]
        im = back[j * PAD : (j + 1) * PAD, BLOCK:]
        out_re = turn[0] * re + turn[1] * im
        out_im = turn[0] * im - turn[1] * re
        unturned.append(jnp.concatenate([out_re, out_im], axis=0).astype(jnp.bfloat16))
    return dot32(final[...], jnp.concatenate(unturned, axis=1))


def tick(
    x_hbm, filter_hbm, short_hbm, skip_hbm, outer_hbm, forward_hbm, inverse_hbm, turn_hbm, final_hbm, o_hbm,
    x, kern, short, skip, outer, forward, inverse, turn, final,
    edge, halo, edge_squares, halo_squares, squares, other_squares, root, root_in, short_in, skip_in, kern_early,
    taps, normed, moved, moved_in, shifted_in, query, base, kern_out, kern_in, kern_wide, filt,
    product, got, wide, result, ready, conv, finished, finished_in, out,
    met, load_sem, edge_send, edge_recv, sq_send, sq_recv, small_send, small_recv, move_send, move_recv,
    kern_send, kern_recv, prod_send, prod_recv, conv_send, conv_recv, hop_send, hop_recv, out_sem,
):
    rows, chans = x.shape
    part = chans // HALVES
    section, ctx, tp = lax.axis_index("section"), lax.axis_index("ctx"), lax.axis_index("tp")
    n_section = lax.axis_size("section")
    z, y = ctx // SIDE, ctx % SIDE
    following, before = (ctx + 1) % HALF, (ctx + HALF - 1) % HALF
    onward = (section + 1) % n_section

    pairs = (
        (x_hbm, x), (filter_hbm, kern), (short_hbm, short), (skip_hbm, skip), (outer_hbm, outer),
        (forward_hbm, forward), (inverse_hbm, inverse), (turn_hbm, turn), (final_hbm, final),
    )
    loads = [pltpu.make_async_copy(src, dst, load_sem.at[i]) for i, (src, dst) in enumerate(pairs)]
    for load in loads:
        load.start()

    barrier = pltpu.get_barrier_semaphore()

    def greet(sem, **to):
        pl.semaphore_signal(sem, inc=1, device_id=to, device_id_type=MESH)

    greet(barrier, tp=1 - tp)
    greet(barrier, ctx=before, tp=0)
    greet(barrier, ctx=before, tp=1)
    for k in range(1, SIDE):
        greet(barrier, ctx=(z + k) % SIDE * SIDE + y)
        greet(barrier, ctx=z * SIDE + (y + k) % SIDE)
    greet(barrier, section=(section + n_section - 1) % n_section)

    loads[0].wait()
    edge[...] = x[rows - HALO :, :]
    total = jnp.zeros((rows, BLOCK), jnp.float32)
    for j in range(chans // BLOCK):
        piece = x[:, j * BLOCK : (j + 1) * BLOCK]
        total = total + piece * piece
    squares[...] = total
    edge_squares[...] = total[rows - HALO :]
    pl.semaphore_wait(barrier, 2 * (SIDE - 1) + 4)

    def remote(src, dst, send, recv, **to):
        return pltpu.make_async_remote_copy(
            src_ref=src, dst_ref=dst, send_sem=send, recv_sem=recv, device_id=to, device_id_type=MESH
        )

    edges = [
        remote(edge, halo, edge_send.at[0], edge_recv.at[0], ctx=following),
        remote(edge_squares, halo_squares.at[0], edge_send.at[1], edge_recv.at[1], ctx=following),
        remote(edge_squares, halo_squares.at[1], edge_send.at[2], edge_recv.at[2], ctx=following, tp=1 - tp),
    ]
    for send in edges:
        send.start()
    swap = remote(squares, other_squares, sq_send, sq_recv, tp=1 - tp)
    swap.start()
    for k in range(1, SIDE):
        greet(met, ctx=(z + k) % SIDE * SIDE + y)

    for load in loads[1:]:
        load.wait()
    late = pl.ds(part, part)
    smalls = [
        remote(short.at[:, :, late], short_in, small_send.at[0], small_recv.at[0], section=onward),
        remote(skip.at[:, late], skip_in, small_send.at[1], small_recv.at[1], section=onward),
        remote(kern, kern_early, small_send.at[2], small_recv.at[2], section=onward),
        remote(root, root_in, small_send.at[3], small_recv.at[3], section=onward),
    ]
    for send in smalls[:3]:
        send.start()
    for f in range(3):
        taps[0, f] = short[f, :, :part].astype(jnp.float32)

    swap.wait_recv()
    mean = jnp.sum(squares[...] + other_squares[...], axis=1, keepdims=True) / CHAN + 1e-06
    scale = lax.rsqrt(mean)
    for send in edges:
        send.wait_recv()
    edge_mean = jnp.sum(halo_squares[0] + halo_squares[1], axis=1, keepdims=True) / CHAN + 1e-06
    edge_normed = jnp.where(ctx == 0, 0.0, halo[...] * lax.rsqrt(edge_mean))
    normed[TOP - HALO : TOP, :] = edge_normed[:, :part].astype(jnp.bfloat16).astype(jnp.float32)
    edge_late = jnp.concatenate([jnp.zeros((TOP - HALO, part), jnp.float32), edge_normed[:, part:]], axis=0)
    moved[:TOP, :] = edge_late.astype(jnp.bfloat16)
    for j in range(part // BLOCK):
        lanes = slice(part + j * BLOCK, part + (j + 1) * BLOCK)
        moved[TOP:, j * BLOCK : (j + 1) * BLOCK] = (x[:, lanes] * scale).astype(jnp.bfloat16)

    def move(row):
        lanes = pl.ds(pl.multiple_of(row * BLOCK, BLOCK), BLOCK)
        return remote(moved.at[:, lanes], moved_in.at[:, lanes], move_send, move_recv.at[row], section=onward)

    def lane_row(i):
        return (z + i * 3) % SIDE

    def start_move(i, carry):
        move(lane_row(i)).start()
        return carry

    lax.fori_loop(0, SIDE, start_move, 0)
    for j in range(part // BLOCK):
        lanes = slice(j * BLOCK, (j + 1) * BLOCK)
        normed[TOP:, lanes] = (x[:, lanes] * scale).astype(jnp.bfloat16).astype(jnp.float32)
    pl.semaphore_wait(met, SIDE - 1)

    def features(h, lanes, shifted, gain):
        made = []
        for f in range(3):
            running = taps[h, f, pl.ds(0, 1), lanes] * shifted[0]
            for t in range(1, TAPS):
                running = running + taps[h, f, pl.ds(t, 1), lanes] * shifted[t]
            made.append(running)
        ask = made[0].astype(jnp.bfloat16).astype(jnp.float32)
        gated = (made[1] * made[2]).astype(jnp.bfloat16).astype(jnp.float32)
        return ask, gated, ask * (gain * gated)

    def send_products(h, row, gated, first):
        product[h, pl.ds(row * SIDE, SIDE)] = gated.T.astype(jnp.bfloat16).reshape(SIDE, GROUP, BLOCK)

        def send(r, inner):
            to = row * SIDE + (y + r) % SIDE
            remote(product.at[h, to], got.at[h, ctx], prod_send.at[h], prod_recv.at[h], ctx=to).start()
            return inner

        lax.fori_loop(jnp.where(first, 1, 0), SIDE, send, 0)

    def early_chunk(i, carry):
        row = lane_row(i)
        lanes = pl.ds(pl.multiple_of(row * BLOCK, BLOCK), BLOCK)
        shifted = [normed[pl.ds(TOP - t, rows), lanes] for t in range(TAPS)]
        ask, gated, direct = features(0, lanes, shifted, skip[:, lanes])
        query[0, :, lanes] = ask
        base[0, :, lanes] = x[:, lanes] + direct
        send_products(0, row, gated, i == 0)
        return carry

    lax.fori_loop(0, SIDE, early_chunk, 0)
    pltpu.make_async_copy(product.at[0, ctx], got.at[0, ctx], prod_recv.at[0]).start()

    root[...] = jnp.broadcast_to(jnp.sqrt(mean), (rows, BLOCK)).T[:SIDE]
    smalls[3].start()
    smalls[2].wait_recv()
    kern_wide[:, 0, :] = kern[...].astype(jnp.float32).T[:HALF]
    kern_wide[:, 1, :] = kern_early[...].astype(jnp.float32).T[HALF:]
    kern_out[...] = kern_wide[...].astype(jnp.bfloat16)

    def at(dz, dy):
        return (z + dz) % SIDE * SIDE + (y + dy) % SIDE

    def send_kern(k, carry):
        to = at(k // SIDE, k % SIDE)
        remote(kern_out.at[to], kern_in.at[ctx], kern_send, kern_recv, ctx=to).start()
        return carry

    lax.fori_loop(1, HALF, send_kern, 0)
    pltpu.make_async_copy(kern_out.at[ctx], kern_in.at[ctx], kern_recv).start()

    for i in (0, 1, 3):
        smalls[i].wait_recv()
    for f in range(3):
        taps[1, f] = short_in[f].astype(jnp.float32)
    spread = jnp.broadcast_to(root_in[0:1, :], (rows, BLOCK)).T

    def wait_in(dst, sem):
        pltpu.make_async_copy(dst, dst, sem).wait()

    def late_chunk(i, carry):
        row = lane_row(i)
        lanes = pl.ds(pl.multiple_of(row * BLOCK, BLOCK), BLOCK)
        wait_in(moved_in.at[:, lanes], move_recv.at[row])
        shifted_in[...] = moved_in[:, lanes].astype(jnp.float32)
        shifted = [shifted_in[TOP - t : TOP - t + rows, :] for t in range(TAPS)]
        ask, gated, direct = features(1, lanes, shifted, skip_in[:, lanes])
        query[1, :, lanes] = ask
        base[1, :, lanes] = shifted[0] * spread + direct
        send_products(1, row, gated, i == 0)
        return carry

    lax.fori_loop(0, SIDE, late_chunk, 0)
    pltpu.make_async_copy(product.at[1, ctx], got.at[1, ctx], prod_recv.at[1]).start()

    wait_in(kern_in, kern_recv)
    kern_wide[...] = kern_in[...].astype(jnp.float32)
    spec = transform([kern_wide[:, h, :] for h in range(HALVES)], outer, forward, turn)
    for h in range(HALVES):
        filt[h] = spec[h * PAD : (h + 1) * PAD]

    for h in range(HALVES):
        wait_in(got.at[h], prod_recv.at[h])
        wide[...] = got[h].astype(jnp.float32).reshape(wide.shape)

        def group(g, carry):
            ids = [g * TOGETHER + j for j in range(TOGETHER)]
            slabs = [wide[pl.ds(c, HALF, stride=GROUP), :] for c in ids]
            spec = transform(slabs, outer, forward, turn)
            gain = filt[h]
            made = untransform(spec, TOGETHER, gain[:, :BLOCK], gain[:, BLOCK:], inverse, turn, final)
            for j, c in enumerate(ids):
                result[pl.ds(c, HALF, stride=GROUP), :] = made[:, j * BLOCK : (j + 1) * BLOCK]
            return carry

        lax.fori_loop(0, GROUP // TOGETHER, group, 0, unroll=True)
        ready[h] = result[...].reshape(HALF, GROUP, BLOCK).astype(jnp.bfloat16)

        def send_back(k, carry):
            to = at(k // SIDE * 3, k % SIDE)
            remote(ready.at[h, to], conv.at[h, ctx], conv_send.at[h], conv_recv.at[h, z], ctx=to).start()
            return carry

        lax.fori_loop(1, HALF, send_back, 0)
        pltpu.make_async_copy(ready.at[h, ctx], conv.at[h, ctx], conv_recv.at[h, z]).start()

    def finish(h, row, lanes):
        blocks = pl.ds(row * SIDE, SIDE)
        wait_in(conv.at[h, blocks], conv_recv.at[h, row])
        got_conv = conv[h, blocks].astype(jnp.float32).reshape(BLOCK, BLOCK).T
        return base[h, :, lanes] + query[h, :, lanes] * got_conv

    def back_row(i):
        return (z + SIDE - i * 3 % SIDE) % SIDE

    def finish_early(i, carry):
        row = back_row(i)
        lanes = pl.ds(pl.multiple_of(row * BLOCK, BLOCK), BLOCK)
        finished[:, lanes] = finish(0, row, lanes).astype(jnp.bfloat16)
        remote(finished.at[:, lanes], finished_in.at[:, lanes], hop_send, hop_recv.at[row], section=onward).start()
        return carry

    lax.fori_loop(0, SIDE, finish_early, 0)

    def finish_late(i, carry):
        row = back_row(i)
        lanes = pl.ds(pl.multiple_of(row * BLOCK, BLOCK), BLOCK)
        after = pl.ds(pl.multiple_of(part + row * BLOCK, BLOCK), BLOCK)
        wait_in(finished_in.at[:, lanes], hop_recv.at[row])
        out[:, lanes] = finished_in[:, lanes].astype(jnp.float32)
        pltpu.make_async_copy(out.at[:, lanes], o_hbm.at[:, lanes], out_sem).start()
        out[:, after] = finish(1, row, lanes)
        pltpu.make_async_copy(out.at[:, after], o_hbm.at[:, after], out_sem).start()
        return carry

    lax.fori_loop(0, SIDE, finish_late, 0)

    sent = pl.ds(0, HALF - 1)
    for send in (swap, *edges, *smalls):
        send.wait_send()
    wait_in(moved, move_send)
    wait_in(kern_out.at[sent], kern_send)
    for h in range(HALVES):
        wait_in(product.at[h, sent], prod_send.at[h])
        wait_in(ready.at[h, sent], conv_send.at[h])
    wait_in(finished, hop_send)
    pltpu.make_async_copy(out, o_hbm, out_sem).wait()


def local(section_input, long_filter, short_filter, skip_gain):
    rows, chans = section_input.shape[1:]
    part = chans // HALVES
    args = (section_input[0], long_filter[0], short_filter[0], skip_gain, *tables())
    anywhere = pl.BlockSpec(memory_space=pl.ANY)
    f32, bf16 = jnp.float32, jnp.bfloat16
    dma = pltpu.SemaphoreType.DMA
    blocks = pltpu.VMEM((HALVES, HALF, GROUP, BLOCK), bf16)
    kernels = pltpu.VMEM((HALF, HALVES, BLOCK), bf16)
    scratch = [pltpu.VMEM(arg.shape, arg.dtype) for arg in args] + [
        pltpu.VMEM((HALO, chans), f32),
        pltpu.VMEM((HALO, chans), f32),
        pltpu.VMEM((HALO, BLOCK), f32),
        pltpu.VMEM((2, HALO, BLOCK), f32),
        pltpu.VMEM((rows, BLOCK), f32),
        pltpu.VMEM((rows, BLOCK), f32),
        pltpu.VMEM((SIDE, BLOCK), f32),
        pltpu.VMEM((SIDE, BLOCK), f32),
        pltpu.VMEM((3, TAPS, part), bf16),
        pltpu.VMEM((1, part), f32),
        pltpu.VMEM(args[1].shape, bf16),
        pltpu.VMEM((HALVES, 3, TAPS, part), f32),
        pltpu.VMEM((TOP + rows, part), f32),
        pltpu.VMEM((TOP + rows, part), bf16),
        pltpu.VMEM((TOP + rows, part), bf16),
        pltpu.VMEM((TOP + rows, BLOCK), f32),
        pltpu.VMEM((HALVES, rows, part), f32),
        pltpu.VMEM((HALVES, rows, part), f32),
        kernels, kernels, pltpu.VMEM((HALF, HALVES, BLOCK), f32),
        pltpu.VMEM((HALVES, PAD, 2 * BLOCK), f32),
        blocks, blocks,
        pltpu.VMEM((HALF * GROUP, BLOCK), f32),
        pltpu.VMEM((HALF * GROUP, BLOCK), f32),
        blocks, blocks,
        pltpu.VMEM((rows, part), bf16),
        pltpu.VMEM((rows, part), bf16),
        pltpu.VMEM((rows, chans), f32),
        pltpu.SemaphoreType.REGULAR,
        dma((len(args),)),
        dma((3,)), dma((3,)),
        dma, dma,
        dma((4,)), dma((4,)),
        dma, dma((SIDE,)),
        dma, dma,
        dma((HALVES,)), dma((HALVES,)),
        dma((HALVES,)), dma((HALVES, SIDE)),
        dma, dma((SIDE,)),
        dma,
    ]
    received = pl.pallas_call(
        tick,
        out_shape=jax.ShapeDtypeStruct((rows, chans), f32),
        in_specs=[anywhere] * len(args),
        out_specs=anywhere,
        scratch_shapes=scratch,
        compiler_params=pltpu.CompilerParams(collective_id=0, has_side_effects=True, vmem_limit_bytes=56 << 20),
        name="tick",
    )(*args)
    return received[None]


def solution(mesh):
    in_specs = (
        P("section", "ctx", "tp"),
        P("section", "ctx", "tp"),
        P("section", None, None, "tp"),
        P("section", "tp"),
    )
    out_specs = P("section", "ctx", "tp")
    return jax.shard_map(local, mesh=mesh, in_specs=in_specs, out_specs=out_specs, check_vma=False)
```

time: 56.1 us -> 53.3 us (0.950)
  the two profiles are of different devices: /device:TPU:1 before, /device:TPU:64 now
where the time goes in v4:
time: 53.3 us; the launch traced here: 53.1 us
  Pallas kernels  50.8 us (95%)
  local copies, waits for them, and re-layouts  2.3 us (4%)
    pallas_call x1, Pallas kernels, local(): pl.pallas_call(tick, out_shape=jax.ShapeDtypeStruct((rows, chans), f32),...  50.8 us
    unnamed x1, local copies, waits for them, and re-layouts  2.3 us

profile of v4, /device:TPU:64, one launch (start us, length us, event | category | flops | bytes accessed | tf_op | source)
XLA Modules:
  0.0 53.1 jit_solution(9680407518857624307)
XLA Ops:
  0.0 50.8 %tick.1 = f32[128,2048]{1,0:T(8,128)} custom-call(f32[128,2048]{1,0:T(8,128)} %bitcast.5, bf16[128,128]{1,0:T(8,128)(2,1)} %bitcast.7, bf16[3,3,2048]{2,1,0:T(4,128)(2,1)} %bitcast.6, f32[1,2048]{1,0:T(1,128)} %skip_hbm.1, bf16[160,64]{1,0:T(8,128)(2,1)} %constant.10.clone.outer_hbm, bf16[256,256]{1,0:T(8,128)(2,1)} %constant.11.clone.forward_hbm, ...), custom_call_target="tpu_custom_call" | custom-call | tf_op jit(solution)/shard_map/tick/pallas_call | solution.py:405
  50.8 2.3 %copy.11 = f32[1,128,2048]{2,1,0:T(8,128)} copy(f32[1,128,2048]{2,1,0:T(8,128)} %bitcast.4) | data formatting | bytes 2097152

commit v5 on v4

--- a/solution.py
+++ b/solution.py
@@ -94,13 +94,13 @@
 
 
 def tick(
-    x_hbm, filter_hbm, short_hbm, skip_hbm, outer_hbm, forward_hbm, inverse_hbm, turn_hbm, final_hbm, o_hbm,
+    x_hbm, filter_hbm, short_hbm, skip_hbm, outer_hbm, forward_hbm, inverse_hbm, turn_hbm, final_hbm, out,
     x, kern, short, skip, outer, forward, inverse, turn, final,
     edge, halo, edge_squares, halo_squares, squares, other_squares, root, root_in, short_in, skip_in, kern_early,
     taps, normed, moved, moved_in, shifted_in, query, base, kern_out, kern_in, kern_wide, filt,
-    product, got, wide, result, ready, conv, finished, finished_in, out,
+    product, got, wide, result, ready, conv, finished, finished_in,
     met, load_sem, edge_send, edge_recv, sq_send, sq_recv, small_send, small_recv, move_send, move_recv,
-    kern_send, kern_recv, prod_send, prod_recv, conv_send, conv_recv, hop_send, hop_recv, out_sem,
+    kern_send, kern_recv, prod_send, prod_recv, conv_send, conv_recv, hop_send, hop_recv,
 ):
     rows, chans = x.shape
     part = chans // HALVES
@@ -109,6 +109,7 @@
     z, y = ctx // SIDE, ctx % SIDE
     following, before = (ctx + 1) % HALF, (ctx + HALF - 1) % HALF
     onward = (section + 1) % n_section
+    step_z, step_y = 3 + 2 * tp, 3 + 2 * tp
 
     pairs = (
         (x_hbm, x), (filter_hbm, kern), (short_hbm, short), (skip_hbm, skip), (outer_hbm, outer),
@@ -191,13 +192,8 @@
         return remote(moved.at[:, lanes], moved_in.at[:, lanes], move_send, move_recv.at[row], section=onward)
 
     def lane_row(i):
-        return (z + i * 3) % SIDE
-
-    def start_move(i, carry):
-        move(lane_row(i)).start()
-        return carry
-
-    lax.fori_loop(0, SIDE, start_move, 0)
+        return (z + i * step_z) % SIDE
+
     for j in range(part // BLOCK):
         lanes = slice(j * BLOCK, (j + 1) * BLOCK)
         normed[TOP:, lanes] = (x[:, lanes] * scale).astype(jnp.bfloat16).astype(jnp.float32)
@@ -218,7 +214,7 @@
         product[h, pl.ds(row * SIDE, SIDE)] = gated.T.astype(jnp.bfloat16).reshape(SIDE, GROUP, BLOCK)
 
         def send(r, inner):
-            to = row * SIDE + (y + r) % SIDE
+            to = row * SIDE + (y + r * step_y) % SIDE
             remote(product.at[h, to], got.at[h, ctx], prod_send.at[h], prod_recv.at[h], ctx=to).start()
             return inner
 
@@ -231,6 +227,7 @@
         ask, gated, direct = features(0, lanes, shifted, skip[:, lanes])
         query[0, :, lanes] = ask
         base[0, :, lanes] = x[:, lanes] + direct
+        move(row).start()
         send_products(0, row, gated, i == 0)
         return carry
 
@@ -248,7 +245,7 @@
         return (z + dz) % SIDE * SIDE + (y + dy) % SIDE
 
     def send_kern(k, carry):
-        to = at(k // SIDE, k % SIDE)
+        to = at(k // SIDE * step_z, k % SIDE * step_y)
         remote(kern_out.at[to], kern_in.at[ctx], kern_send, kern_recv, ctx=to).start()
         return carry
 
@@ -303,7 +300,7 @@
         ready[h] = result[...].reshape(HALF, GROUP, BLOCK).astype(jnp.bfloat16)
 
         def send_back(k, carry):
-            to = at(k // SIDE * 3, k % SIDE)
+            to = at(k // SIDE * step_z, k % SIDE * step_y)
             remote(ready.at[h, to], conv.at[h, ctx], conv_send.at[h], conv_recv.at[h, z], ctx=to).start()
             return carry
 
@@ -317,7 +314,7 @@
         return base[h, :, lanes] + query[h, :, lanes] * got_conv
 
     def back_row(i):
-        return (z + SIDE - i * 3 % SIDE) % SIDE
+        return (z + i * (SIDE - step_z)) % SIDE
 
     def finish_early(i, carry):
         row = back_row(i)
@@ -334,9 +331,7 @@
         after = pl.ds(pl.multiple_of(part + row * BLOCK, BLOCK), BLOCK)
         wait_in(finished_in.at[:, lanes], hop_recv.at[row])
         out[:, lanes] = finished_in[:, lanes].astype(jnp.float32)
-        pltpu.make_async_copy(out.at[:, lanes], o_hbm.at[:, lanes], out_sem).start()
         out[:, after] = finish(1, row, lanes)
-        pltpu.make_async_copy(out.at[:, after], o_hbm.at[:, after], out_sem).start()
         return carry
 
     lax.fori_loop(0, SIDE, finish_late, 0)
@@ -350,7 +345,6 @@
         wait_in(product.at[h, sent], prod_send.at[h])
         wait_in(ready.at[h, sent], conv_send.at[h])
     wait_in(finished, hop_send)
-    pltpu.make_async_copy(out, o_hbm, out_sem).wait()
 
 
 def local(section_input, long_filter, short_filter, skip_gain):
@@ -389,7 +383,6 @@
         blocks, blocks,
         pltpu.VMEM((rows, part), bf16),
         pltpu.VMEM((rows, part), bf16),
-        pltpu.VMEM((rows, chans), f32),
         pltpu.SemaphoreType.REGULAR,
         dma((len(args),)),
         dma((3,)), dma((3,)),
@@ -400,17 +393,16 @@
         dma((HALVES,)), dma((HALVES,)),
         dma((HALVES,)), dma((HALVES, SIDE)),
         dma, dma((SIDE,)),
-        dma,
     ]
     received = pl.pallas_call(
         tick,
         out_shape=jax.ShapeDtypeStruct((rows, chans), f32),
         in_specs=[anywhere] * len(args),
-        out_specs=anywhere,
+        out_specs=pl.BlockSpec(memory_space=pltpu.VMEM),
         scratch_shapes=scratch,
-        compiler_params=pltpu.CompilerParams(collective_id=0, has_side_effects=True, vmem_limit_bytes=56 << 20),
+        compiler_params=pltpu.CompilerParams(collective_id=0, has_side_effects=True, vmem_limit_bytes=48 << 20),
         name="tick",
-    )(*args)
+    )(*(pltpu.with_memory_space_constraint(arg, pltpu.HBM) for arg in args))
     return received[None]
 
 

time: 53.3 us -> 50.8 us (0.953)
  the two profiles are of different devices: /device:TPU:64 before, /device:TPU:65 now
where the time goes in v5:
time: 50.8 us; the launch traced here: 50.6 us
  Pallas kernels  49.6 us (98%)
  local copies, waits for them, and re-layouts  0.97 us (2%)
    pallas_call x1, Pallas kernels, local(): pl.pallas_call(tick, out_shape=jax.ShapeDtypeStruct((rows, chans), f32),...  49.6 us

profile of v5, /device:TPU:65, one launch (start us, length us, event | category | flops | bytes accessed | tf_op | source)
XLA Modules:
  0.0 50.6 jit_solution(13725913387620670785)
XLA Ops:
  0.0 49.6 %tick.1 = f32[128,2048]{1,0:T(8,128)S(1)} custom-call(f32[128,2048]{1,0:T(8,128)} %bitcast.5, bf16[128,128]{1,0:T(8,128)(2,1)} %bitcast.7, bf16[3,3,2048]{2,1,0:T(4,128)(2,1)} %bitcast.6, f32[1,2048]{1,0:T(1,128)} %skip_hbm.1, bf16[160,64]{1,0:T(8,128)(2,1)} %constant.10.clone.outer_hbm, bf16[256,256]{1,0:T(8,128)(2,1)} %constant.11.clone.forward_hbm, ...), custom_call_target="tpu_custom_call" | custom-call | tf_op jit(solution)/shard_map/tick/pallas_call | solution.py:397
  49.7 1.0 %copy.11 = f32[1,128,2048]{2,1,0:T(8,128)} copy(f32[1,128,2048]{2,1,0:T(8,128)S(1)} %bitcast.4) | data formatting | bytes 2097152

commit v6 on v5

--- a/solution.py
+++ b/solution.py
@@ -16,7 +16,7 @@
 SPAN = 2 * HALF
 TOTAL = SPAN * BLOCK
 ROWS = HALF + 1
-PAD = 80
+PAD = 72
 SIDE = 8
 TOGETHER = 8
 GROUP = 16
@@ -109,7 +109,7 @@
     z, y = ctx // SIDE, ctx % SIDE
     following, before = (ctx + 1) % HALF, (ctx + HALF - 1) % HALF
     onward = (section + 1) % n_section
-    step_z, step_y = 3 + 2 * tp, 3 + 2 * tp
+    step_z, step_y = 3 + 2 * tp, 5 - 2 * tp
 
     pairs = (
         (x_hbm, x), (filter_hbm, kern), (short_hbm, short), (skip_hbm, skip), (outer_hbm, outer),
@@ -325,15 +325,21 @@
 
     lax.fori_loop(0, SIDE, finish_early, 0)
 
+    def take_early(i, carry):
+        row = back_row(i)
+        lanes = pl.ds(pl.multiple_of(row * BLOCK, BLOCK), BLOCK)
+        wait_in(finished_in.at[:, lanes], hop_recv.at[row])
+        out[:, lanes] = finished_in[:, lanes].astype(jnp.float32)
+        return carry
+
     def finish_late(i, carry):
         row = back_row(i)
         lanes = pl.ds(pl.multiple_of(row * BLOCK, BLOCK), BLOCK)
         after = pl.ds(pl.multiple_of(part + row * BLOCK, BLOCK), BLOCK)
-        wait_in(finished_in.at[:, lanes], hop_recv.at[row])
-        out[:, lanes] = finished_in[:, lanes].astype(jnp.float32)
         out[:, after] = finish(1, row, lanes)
         return carry
 
+    lax.fori_loop(0, SIDE, take_early, 0)
     lax.fori_loop(0, SIDE, finish_late, 0)
 
     sent = pl.ds(0, HALF - 1)

time: 50.8 us -> 50.4 us (level)
  the two profiles are of different devices: /device:TPU:65 before, /device:TPU:8 now
where the time goes in v6:
time: 50.4 us; the launch traced here: 50.3 us
  Pallas kernels  49.3 us (98%)
  local copies, waits for them, and re-layouts  0.97 us (2%)
    pallas_call x1, Pallas kernels, local(): pl.pallas_call(tick, out_shape=jax.ShapeDtypeStruct((rows, chans), f32),...  49.3 us

profile of v6, /device:TPU:8, one launch (start us, length us, event | category | flops | bytes accessed | tf_op | source)
XLA Modules:
  0.0 50.3 jit_solution(8095098676199414155)
XLA Ops:
  0.0 49.3 %tick.1 = f32[128,2048]{1,0:T(8,128)S(1)} custom-call(f32[128,2048]{1,0:T(8,128)} %bitcast.5, bf16[128,128]{1,0:T(8,128)(2,1)} %bitcast.7, bf16[3,3,2048]{2,1,0:T(4,128)(2,1)} %bitcast.6, f32[1,2048]{1,0:T(1,128)} %skip_hbm.1, bf16[144,64]{1,0:T(8,128)(2,1)} %constant.10.clone.outer_hbm, bf16[256,256]{1,0:T(8,128)(2,1)} %constant.11.clone.forward_hbm, ...), custom_call_target="tpu_custom_call" | custom-call | tf_op jit(solution)/shard_map/tick/pallas_call | solution.py:403
  49.3 1.0 %copy.11 = f32[1,128,2048]{2,1,0:T(8,128)} copy(f32[1,128,2048]{2,1,0:T(8,128)S(1)} %bitcast.4) | data formatting | bytes 2097152

commit v7 on v6

--- a/solution.py
+++ b/solution.py
@@ -109,7 +109,7 @@
     z, y = ctx // SIDE, ctx % SIDE
     following, before = (ctx + 1) % HALF, (ctx + HALF - 1) % HALF
     onward = (section + 1) % n_section
-    step_z, step_y = 3 + 2 * tp, 5 - 2 * tp
+    step_z, step_y = 7 - 6 * tp, 3 + 2 * tp
 
     pairs = (
         (x_hbm, x), (filter_hbm, kern), (short_hbm, short), (skip_hbm, skip), (outer_hbm, outer),

time: 50.4 us -> 50.2 us (level)
  the two profiles are of different devices: /device:TPU:8 before, /device:TPU:66 now
where the time goes in v7:
time: 50.2 us; the launch traced here: 50.1 us
  Pallas kernels  49.1 us (98%)
  local copies, waits for them, and re-layouts  0.97 us (2%)
    pallas_call x1, Pallas kernels, local(): pl.pallas_call(tick, out_shape=jax.ShapeDtypeStruct((rows, chans), f32),...  49.1 us

profile of v7, /device:TPU:66, one launch (start us, length us, event | category | flops | bytes accessed | tf_op | source)
XLA Modules:
  0.0 50.1 jit_solution(12923745668616489502)
XLA Ops:
  0.0 49.1 %tick.1 = f32[128,2048]{1,0:T(8,128)S(1)} custom-call(f32[128,2048]{1,0:T(8,128)} %bitcast.5, bf16[128,128]{1,0:T(8,128)(2,1)} %bitcast.7, bf16[3,3,2048]{2,1,0:T(4,128)(2,1)} %bitcast.6, f32[1,2048]{1,0:T(1,128)} %skip_hbm.1, bf16[144,64]{1,0:T(8,128)(2,1)} %constant.10.clone.outer_hbm, bf16[256,256]{1,0:T(8,128)(2,1)} %constant.11.clone.forward_hbm, ...), custom_call_target="tpu_custom_call" | custom-call | tf_op jit(solution)/shard_map/tick/pallas_call | solution.py:403
  49.1 1.0 %copy.11 = f32[1,128,2048]{2,1,0:T(8,128)} copy(f32[1,128,2048]{2,1,0:T(8,128)S(1)} %bitcast.4) | data formatting | bytes 2097152

commit v8 on v7

--- a/solution.py
+++ b/solution.py
@@ -109,7 +109,7 @@
     z, y = ctx // SIDE, ctx % SIDE
     following, before = (ctx + 1) % HALF, (ctx + HALF - 1) % HALF
     onward = (section + 1) % n_section
-    step_z, step_y = 7 - 6 * tp, 3 + 2 * tp
+    step_z, step_y = 7 - 6 * tp, 7 - 6 * tp
 
     pairs = (
         (x_hbm, x), (filter_hbm, kern), (short_hbm, short), (skip_hbm, skip), (outer_hbm, outer),

time: 50.2 us -> 50 us (level)
  the two profiles are of different devices: /device:TPU:66 before, /device:TPU:1 now
where the time goes in v8:
time: 50 us; the launch traced here: 49.2 us
  Pallas kernels  48.2 us (96%)
  local copies, waits for them, and re-layouts  0.97 us (2%)
    pallas_call x1, Pallas kernels, local(): pl.pallas_call(tick, out_shape=jax.ShapeDtypeStruct((rows, chans), f32),...  48.2 us

profile of v8, /device:TPU:1, one launch (start us, length us, event | category | flops | bytes accessed | tf_op | source)
XLA Modules:
  0.0 49.2 jit_solution(9362179731754547020)
XLA Ops:
  0.0 48.2 %tick.1 = f32[128,2048]{1,0:T(8,128)S(1)} custom-call(f32[128,2048]{1,0:T(8,128)} %bitcast.5, bf16[128,128]{1,0:T(8,128)(2,1)} %bitcast.7, bf16[3,3,2048]{2,1,0:T(4,128)(2,1)} %bitcast.6, f32[1,2048]{1,0:T(1,128)} %skip_hbm.1, bf16[144,64]{1,0:T(8,128)(2,1)} %constant.10.clone.outer_hbm, bf16[256,256]{1,0:T(8,128)(2,1)} %constant.11.clone.forward_hbm, ...), custom_call_target="tpu_custom_call" | custom-call | tf_op jit(solution)/shard_map/tick/pallas_call | solution.py:403
  48.2 1.0 %copy.11 = f32[1,128,2048]{2,1,0:T(8,128)} copy(f32[1,128,2048]{2,1,0:T(8,128)S(1)} %bitcast.4) | data formatting | bytes 2097152
